TPU v7x, 32 devices: a whole 2x2x4 slice. The times are simulated.
32 devices in a mesh: tbl: 8 (over z, y), pair: 4 (over x, core).
Axes of the slice: x: 2, y: 2, z: 4, core: 2. Of those that a mesh axis runs over, the one named last changes fastest.
Arguments:
- codes: bfloat16 [112, 64, 16384], P('tbl', None, 'pair'), may hold values from -127 to 127
- scales: float32 [112, 16384], P('tbl', 'pair'), may hold values from 0.002 to 0.02
- shard_slot: int32 [8, 14], replicated, may hold values from -1 to 53, as said below
- weight_first: bfloat16 [351, 1024], replicated, may hold values from -0.3125 to 0.3125
- bias_first: float32 [1024], replicated, may hold values from -3 to 3
- weight_second: bfloat16 [1024, 1024], replicated, may hold values from -0.1875 to 0.1875
- bias_second: float32 [1024], replicated, may hold values from -3 to 3
- weight_third: bfloat16 [1024, 512], replicated, may hold values from -0.1875 to 0.1875
- bias_third: float32 [512], replicated, may hold values from -3 to 3
- weight_fourth: bfloat16 [512, 256], replicated, may hold values from -0.25 to 0.25
- bias_fourth: float32 [256], replicated, may hold values from -3 to 3
- weight_out: bfloat16 [256], replicated, may hold values from -0.375 to 0.375
- bias_out: float32 [1], replicated, may hold values from -3 to 3
Outputs:
- logits: float32 [4, 4096], P(None, 'tbl')
Inputs may be any that keep to these rules, and one draw needn't show every extreme that they name: `shard_slot`: each shard 0 to 53 stands in exactly one slot; all other slots hold -1. For k below half of the tbl size, row k holds its shards in its first slots and the row half the tbl size further holds its shards in its last slots, and the two rows hold 14 shards or fewer together. Some row holds 14 shards.
All inputs are finite; a program needn't handle non-finite values.
Results may differ from a plain program's by a relative error of at most 0.03.
Values may be sent and summed in bfloat16 or wider, within the bound.
No kernel may reach another device: no remote copies, remote signals or barrier semaphores. Data moves between devices by JAX's collectives and lax.ppermute only.
A program may use at most 128 MiB of HBM per device.

v0:
```python
import functools
import jax
import jax.numpy as jnp
from jax import lax
from jax.experimental import pallas as pl
from jax.experimental.pallas import tpu as pltpu
from jax.sharding import PartitionSpec as P

TABLES = 27
LANES = 128
CHUNK = 6
ROUND_STEPS = (12, 13, 15)
LAG = 2
PIECE_AFTER = (0, 2, 4, 6)
PIECE_ROUND = (3, 5, 7, 10)
SPAN = 256


def piece_order(nodes, node):
    if node < nodes // 2:
        return tuple(range(nodes - 1, node, -1)) + tuple(range(node)) + (node,)
    return tuple(range(node)) + tuple(range(nodes - 1, node, -1)) + (node,)


def whole_chunks(value):
    return (value * (-(-65536 // CHUNK))) >> 16


class Codes:
    def __init__(self, nodes, slots):
        self.nodes, self.slots = nodes, slots
        self.piece = 2 * nodes * slots
        self.pool = self.piece + nodes * slots
        self.units = nodes * nodes * slots
        self.stage = self.pool + self.units
        self.pool_rows = self.units + 2 * CHUNK


def time_lists(code, counts, column, ends):
    nodes, slots = code.nodes, code.slots
    half = nodes // 2
    rows = {}
    for place in range(nodes):
        for other in range(2):
            row = column if other == 0 else 1 - column
            count = jnp.where(row == 0, counts[2 * place], counts[2 * place + 1])
            first = 0 if place < half else slots - count
            rows[place, other] = (count, first, ((place % half) * 2 + row) * slots)

    lists = {}
    for up in (True, False):
        starts = {}
        path = range(nodes - 1) if up else range(nodes - 1, 0, -1)
        for place in path:
            goals = range(nodes - 1, place, -1) if up else range(place)
            before = range(place - 1, -1, -1) if up else range(place + 1, nodes)
            pieces = piece_order(nodes, place)
            items = [(source, other, goal) for other in range(2) for goal in goals for source in (place, *before)]
            end, here, segments = jnp.int32(0), {}, []
            for source, other, goal in items:
                count, first, _ = rows[source, other]
                if source != place:
                    ready = starts[source, other, goal] + LAG * CHUNK
                elif other:
                    ready = jnp.int32(PIECE_ROUND[pieces.index(goal)] * CHUNK)
                else:
                    ready = jnp.int32(0)
                start = jnp.maximum(end, ready)
                segments.append((source, other, goal, start, starts.get((source, other, goal))))
                here[source, other, goal] = start
                end = jnp.where(count > 0, start + count, end)
            lists[up, place] = segments
            ends.append(end)
            starts = here
    return rows, lists


def plan_kernel(code, slot_ref, me_ref, out_ref):
    nodes, slots = code.nodes, code.slots
    me = me_ref[0]
    column, node = me & 1, me >> 1
    counts = []
    for row in range(2 * nodes):
        total = jnp.int32(0)
        for slot in range(slots):
            total += (slot_ref[row, slot] >= 0).astype(jnp.int32)
        counts.append(total)
    ends = []
    for flip in range(2):
        rows, lists = time_lists(code, counts, column ^ flip, ends)
        if flip == 0:
            own_rows, own_lists = rows, lists
    rows, lists = own_rows, own_lists
    last = functools.reduce(jnp.maximum, ends)

    spot = lax.broadcasted_iota(jnp.int32, (1, SPAN), 1)
    turn_of = whole_chunks(spot)
    rest = spot - turn_of * CHUNK
    tables = {}
    for (up, place), segments in lists.items():
        side = place % 2 if up else (place - 1) % 2
        came = 1 - side
        send = jnp.zeros((1, SPAN), jnp.int32)
        unit = code.units + side * CHUNK + rest
        for source, other, goal, start, earlier in segments:
            count, first, base = rows[source, other]
            index = spot - start
            inside = (index >= 0) & (index < count)
            slot = first + index
            this = goal * nodes * slots + base + slot
            if source != place:
                arrived = earlier + index
                came_in = whole_chunks(arrived)
                staged = code.stage + came * CHUNK + arrived - came_in * CHUNK
                origin = jnp.where(turn_of - came_in == LAG, staged, code.pool + this)
            elif other:
                origin = code.piece + piece_order(nodes, place).index(goal) * slots + slot
            else:
                origin = (goal * 2 + column) * slots + slot
            send = jnp.where(inside, origin, send)
            unit = jnp.where(inside, this, unit)
        tables[up, place] = (send, unit)
    blank = jnp.zeros((1, SPAN), jnp.int32)
    for side in range(2):
        sent = blank
        kept = code.units + side * CHUNK + rest
        for place in range(nodes):
            up = place % 2 == side
            peer = place + 1 if up else place - 1
            if 0 <= peer < nodes:
                sent = jnp.where(node == place, tables[up, place][0], sent)
                kept = jnp.where(node == place, tables[not up, peer][1], kept)
        out_ref[side:side + 1, :] = sent
        out_ref[2 + side:3 + side, :] = kept
    out_ref[4:5, :] = blank + lax.div(last + CHUNK - 1, jnp.int32(CHUNK))
    places = blank
    for row in range(2 * nodes):
        base = code.pool + (node * nodes + row % nodes) * slots
        base = jnp.where(row == (me ^ 1), code.piece, base)
        base = jnp.where(row == me, me * slots, base)
        for slot in range(slots):
            places = jnp.where(spot == slot_ref[row, slot], base + slot, places)
    out_ref[5:6, :] = places
    out_ref[6:8, :] = jnp.zeros((2, SPAN), jnp.int32)


def plan(shard_slot, me, code):
    return pl.pallas_call(
        functools.partial(plan_kernel, code),
        out_shape=jax.ShapeDtypeStruct((8, SPAN), jnp.int32),
        in_specs=[pl.BlockSpec(memory_space=pltpu.SMEM)] * 2,
        out_specs=pl.BlockSpec(memory_space=pltpu.VMEM),
        name="plan",
    )(shard_slot, me)


def rescale(block, scales_ref, slot, start, count):
    factor = scales_ref[pl.ds(slot, 1), pl.ds(pl.multiple_of(start, LANES), count)]
    return (block.astype(jnp.float32) * factor).astype(block.dtype)


def turn_kernel(code, n_pieces, has_pool, has_recv, base, table_ref, *refs):
    refs = list(refs)
    if base is None:
        base = refs.pop(0)[0] * CHUNK
    codes_ref, scales_ref = refs.pop(0), refs.pop(0)
    pieces = [refs.pop(0) for _ in range(n_pieces)]
    if has_pool:
        refs.pop(0)
    recvs = [refs.pop(0) for _ in range(2)] if has_recv else []
    pool_ref, send_a, send_b, buf, load_sem, recv_sem, pool_sem = refs
    slots = code.slots
    count = buf.shape[2]
    loads = [pltpu.make_async_copy(ref, buf.at[pl.ds(s * CHUNK, CHUNK)], recv_sem.at[s]) for s, ref in enumerate(recvs)]

    def gather(side, send, c, carry):
        e = table_ref[side, base + c]
        goal = send.at[c]

        @pl.when(e < code.piece)
        def _():
            dest = lax.div(e, jnp.int32(slots))
            lanes = pl.ds(pl.multiple_of(dest * count, count), count)
            pltpu.make_async_copy(codes_ref.at[e - dest * slots, :, lanes], goal, load_sem).start()

        if has_recv:
            @pl.when(e >= code.piece)
            def _():
                for n, piece in enumerate(pieces):
                    low = code.piece + n * slots

                    @pl.when((e >= low) & (e < low + slots))
                    def _():
                        pltpu.make_async_copy(piece.at[e - low], goal, load_sem).start()

                @pl.when((e >= code.pool) & (e < code.stage))
                def _():
                    pltpu.make_async_copy(pool_ref.at[e - code.pool], goal, load_sem).start()

                for n, recv in enumerate(recvs):
                    low = code.stage + n * CHUNK

                    @pl.when((e >= low) & (e < low + CHUNK))
                    def _():
                        pltpu.make_async_copy(recv.at[e - low], goal, load_sem).start()

        return carry

    def gathered(send, c, carry):
        pltpu.make_async_copy(codes_ref.at[0, :, pl.ds(0, count)], send.at[c], load_sem).wait()
        return carry

    def keep(side, c, carry):
        row = table_ref[2 + side, base - LAG * CHUNK + c]
        pltpu.make_async_copy(buf.at[side * CHUNK + c], pool_ref.at[row], pool_sem).start()
        return carry

    def kept(c, carry):
        pltpu.make_async_copy(buf.at[0], pool_ref.at[0], pool_sem).wait()
        return carry

    def scale(side, send, c, carry):
        e = table_ref[side, base + c]

        @pl.when(e < code.piece)
        def _():
            dest = lax.div(e, jnp.int32(slots))
            send[c] = rescale(send[c], scales_ref, e - dest * slots, dest * count, count)

        return carry

    sides = ((0, send_a), (1, send_b))
    for side, send in sides:
        lax.fori_loop(0, CHUNK, functools.partial(gather, side, send), 0)
    for copy in loads:
        copy.start()
    for side, send in sides:
        lax.fori_loop(0, CHUNK, functools.partial(gathered, send), 0)
    if has_recv:
        for side in range(2):
            loads[side].wait()
            lax.fori_loop(0, CHUNK, functools.partial(keep, side), 0)
    for side, send in sides:
        lax.fori_loop(0, CHUNK, functools.partial(scale, side, send), 0)
    if has_recv:
        lax.fori_loop(0, 2 * CHUNK, kept, 0)


def turn(code, table, number, codes, scales, pieces, pool, recv, count):
    half = codes.shape[1]
    anywhere = pl.BlockSpec(memory_space=pl.ANY)
    vmem = pl.BlockSpec(memory_space=pltpu.VMEM)
    block = jax.ShapeDtypeStruct((CHUNK, half, count), codes.dtype)
    operands = [codes, scales, *pieces] + ([] if pool is None else [pool]) + list(recv or ())
    specs = [anywhere, vmem] + [anywhere] * (len(operands) - 2)
    fixed = isinstance(number, int)
    scalars = (table,) if fixed else (table, number)
    aliases = {} if pool is None else {len(scalars) + 2 + len(pieces): 0}
    size = CHUNK * half * count * 2
    base = number * CHUNK if fixed else None
    return pl.pallas_call(
        functools.partial(turn_kernel, code, len(pieces), pool is not None, recv is not None, base),
        out_shape=(jax.ShapeDtypeStruct((code.pool_rows, half, count), codes.dtype), block, block),
        grid_spec=pltpu.PrefetchScalarGridSpec(
            num_scalar_prefetch=len(scalars),
            grid=(),
            in_specs=specs,
            out_specs=(anywhere, vmem, vmem),
            scratch_shapes=[
                pltpu.VMEM((2 * CHUNK, half, count), codes.dtype),
                pltpu.SemaphoreType.DMA,
                pltpu.SemaphoreType.DMA((2,)),
                pltpu.SemaphoreType.DMA,
            ],
        ),
        input_output_aliases=aliases,
        compiler_params=pltpu.CompilerParams(vmem_limit_bytes=8 << 20),
        cost_estimate=pl.CostEstimate(flops=size, bytes_accessed=8 * size, transcendentals=0),
        name="turn",
    )(*scalars, *operands)


def piece_kernel(nodes, n, me_ref, codes_ref, scales_ref, after_ref, out_ref, sem):
    me = me_ref[0]
    goal = jnp.int32(0)
    for place in range(nodes):
        goal = jnp.where((me >> 1) == place, piece_order(nodes, place)[n], goal)
    slots, _, count = out_ref.shape
    start = pl.multiple_of((goal * 2 + 1 - (me & 1)) * count, count)
    copy = pltpu.make_async_copy(codes_ref.at[:, :, pl.ds(start, count)], out_ref, sem)
    copy.start()
    copy.wait()

    def scale(slot, carry):
        out_ref[slot] = rescale(out_ref[slot], scales_ref, slot, start, count)
        return carry

    lax.fori_loop(0, slots, scale, 0)


def column_piece(nodes, n, me, codes, scales, after, count):
    slots, half, _ = codes.shape
    anywhere = pl.BlockSpec(memory_space=pl.ANY)
    vmem = pl.BlockSpec(memory_space=pltpu.VMEM)
    return pl.pallas_call(
        functools.partial(piece_kernel, nodes, n),
        out_shape=jax.ShapeDtypeStruct((slots, half, count), codes.dtype),
        grid_spec=pltpu.PrefetchScalarGridSpec(
            num_scalar_prefetch=1,
            grid=(),
            in_specs=[anywhere, vmem, anywhere],
            out_specs=vmem,
            scratch_shapes=[pltpu.SemaphoreType.DMA],
        ),
        compiler_params=pltpu.CompilerParams(vmem_limit_bytes=8 << 20),
        cost_estimate=pl.CostEstimate(flops=slots * half * count, bytes_accessed=4 * slots * half * count, transcendentals=0),
        name="piece",
    )(me, codes, scales, after)


def settle_kernel(table_ref, round_ref, pool_in, recv_a, recv_b, pool_ref, buf, load_sem, pool_sem):
    base = round_ref[0] * CHUNK
    loads = [pltpu.make_async_copy(ref, buf.at[pl.ds(n * CHUNK, CHUNK)], load_sem.at[n]) for n, ref in enumerate((recv_a, recv_b))]
    for copy in loads:
        copy.start()
    stores = []
    for n in range(2):
        loads[n].wait()
        for c in range(CHUNK):
            row = table_ref[2 + n, base + c]
            stores.append(pltpu.make_async_copy(buf.at[n * CHUNK + c], pool_ref.at[row], pool_sem))
            stores[-1].start()
    for copy in stores:
        copy.wait()


def settle(table, number, pool, recv):
    anywhere = pl.BlockSpec(memory_space=pl.ANY)
    return pl.pallas_call(
        settle_kernel,
        out_shape=jax.ShapeDtypeStruct(pool.shape, pool.dtype),
        grid_spec=pltpu.PrefetchScalarGridSpec(
            num_scalar_prefetch=2,
            grid=(),
            in_specs=[anywhere] * 3,
            out_specs=anywhere,
            scratch_shapes=[
                pltpu.VMEM((2 * CHUNK,) + pool.shape[1:], pool.dtype),
                pltpu.SemaphoreType.DMA((2,)),
                pltpu.SemaphoreType.DMA,
            ],
        ),
        input_output_aliases={2: 0},
        compiler_params=pltpu.CompilerParams(vmem_limit_bytes=8 << 20),
        name="settle",
    )(table, number, pool, *recv)


def score_kernel(limits, pos_ref, pool_ref, codes_ref, piece_ref, scales_ref, *refs):
    sources, refs = refs[:9], refs[9:]
    bo_ref, out_ref, picked, wide, inter = refs[:5]
    copies, (pick_sem, weight_sem) = refs[5:14], refs[14:]
    w1, w2, w3, w4, b1_ref, b2_ref, b3_ref, b4_ref, wo_ref = copies
    shards, half, count = picked.shape
    tables = shards // 2
    weights = [pltpu.make_async_copy(src, dst, weight_sem.at[n]) for n, (src, dst) in enumerate(zip(sources, copies))]

    slots, piece_base, pool_base, table_row = limits

    def begin(shard, carry):
        e = pos_ref[table_row, shard]
        dest = lax.div(e, jnp.int32(slots))

        @pl.when(e < piece_base)
        def _():
            lanes = pl.ds(pl.multiple_of(dest * count, count), count)
            pltpu.make_async_copy(codes_ref.at[e - dest * slots, :, lanes], picked.at[shard], pick_sem).start()

        @pl.when((e >= piece_base) & (e < pool_base))
        def _():
            pltpu.make_async_copy(piece_ref.at[e - piece_base], picked.at[shard], pick_sem).start()

        @pl.when(e >= pool_base)
        def _():
            pltpu.make_async_copy(pool_ref.at[e - pool_base], picked.at[shard], pick_sem).start()

        return carry

    def finish(shard, carry):
        pltpu.make_async_copy(pool_ref.at[0], picked.at[shard], pick_sem).wait()
        return carry

    def rescale(shard, carry):
        e = pos_ref[table_row, shard]
        dest = lax.div(e, jnp.int32(slots))

        @pl.when(e < piece_base)
        def _():
            lanes = pl.ds(pl.multiple_of(dest * count, count), count)
            factor = scales_ref[pl.ds(e - dest * slots, 1), lanes]
            picked[shard] = (picked[shard].astype(jnp.float32) * factor).astype(picked.dtype)

        return carry

    lax.fori_loop(0, shards, begin, 0)
    for copy in weights:
        copy.start()
    lax.fori_loop(0, shards, finish, 0)
    lax.fori_loop(0, shards, rescale, 0)

    def gram_block(block, carry):
        lanes = pl.ds(pl.multiple_of(block * LANES, LANES), LANES)
        for shard in range(shards):
            wide[shard // 2, (shard % 2) * half:(shard % 2 + 1) * half, :] = picked[shard, :, lanes].astype(jnp.float32)
        row = 0
        for i in range(tables):
            left = wide[i]
            for j in range(i + 1, tables):
                inter[row:row + 1, lanes] = jnp.sum(left * wide[j], axis=0, keepdims=True)
                row += 1
        return carry

    lax.fori_loop(0, count // LANES, gram_block, 0)
    for copy in weights:
        copy.wait()
    step = 2 * LANES if count % (2 * LANES) == 0 else LANES

    def dense(hidden, weight, bias):
        product = jnp.dot(hidden, weight[...], preferred_element_type=jnp.float32)
        return jnp.maximum(product + bias[...], 0.0).astype(jnp.bfloat16)

    def top_block(block, carry):
        lanes = pl.ds(pl.multiple_of(block * step, step), step)
        hidden = jnp.transpose(inter[:, lanes]).astype(jnp.bfloat16)
        hidden = dense(hidden, w1, b1_ref)
        hidden = dense(hidden, w2, b2_ref)
        hidden = dense(hidden, w3, b3_ref)
        hidden = dense(hidden, w4, b4_ref)
        final = lax.dot_general(wo_ref[...], hidden, (((1,), (1,)), ((), ())), preferred_element_type=jnp.float32)
        out_ref[:, lanes] = final[0:1] + bo_ref[0]
        return carry

    lax.fori_loop(0, count // step, top_block, 0)


def score(pool, codes, piece, scales, positions, shards, limits, layers):
    (w1, b1), (w2, b2), (w3, b3), (w4, b4), (wo, bo) = layers
    half, count = pool.shape[1:]
    rows = w1.shape[0]
    wo = wo[None, :]
    anywhere = pl.BlockSpec(memory_space=pl.ANY)
    vmem = pl.BlockSpec(memory_space=pltpu.VMEM)
    flops = 2 * count * sum(w.size for w in (w1, w2, w3, w4))
    parts = (w1, w2, w3, w4, b1[None, :], b2[None, :], b3[None, :], b4[None, :], wo)
    return pl.pallas_call(
        functools.partial(score_kernel, limits),
        out_shape=jax.ShapeDtypeStruct((1, count), jnp.float32),
        grid_spec=pltpu.PrefetchScalarGridSpec(
            num_scalar_prefetch=1,
            grid=(),
            in_specs=[anywhere] * 3 + [vmem] + [pl.BlockSpec(memory_space=pltpu.HBM)] * 9 + [pl.BlockSpec(memory_space=pltpu.SMEM)],
            out_specs=vmem,
            scratch_shapes=[
                pltpu.VMEM((shards, half, count), pool.dtype),
                pltpu.VMEM((shards // 2, 2 * half, LANES), jnp.float32),
                pltpu.VMEM((rows, count), jnp.float32),
                *(pltpu.VMEM(part.shape, part.dtype) for part in parts),
                pltpu.SemaphoreType.DMA,
                pltpu.SemaphoreType.DMA((len(parts),)),
            ],
        ),
        compiler_params=pltpu.CompilerParams(vmem_limit_bytes=20 << 20),
        cost_estimate=pl.CostEstimate(flops=flops, bytes_accessed=shards * half * count * 2, transcendentals=0),
        name="score",
    )(positions, pool, codes, piece, scales, *parts, bo)


def shard_positions(slot_table, shard_total):
    flat = slot_table.reshape(-1)
    matches = flat[None, :] == jnp.arange(shard_total, dtype=jnp.int32)[:, None]
    places = jnp.arange(flat.shape[0], dtype=jnp.int32)[None, :]
    return jnp.sum(jnp.where(matches, places, 0), axis=1)


def exchange_all(codes, scales):
    slot_count, half, samples = codes.shape
    tbl_count = lax.axis_size("tbl")
    count = samples // tbl_count
    values = (codes.astype(jnp.float32) * scales[:, None, :]).astype(codes.dtype)
    packed = values.reshape(slot_count, half, tbl_count, count).transpose(2, 0, 1, 3)
    received = lax.all_to_all(packed, "tbl", split_axis=0, concat_axis=0, tiled=True)
    return received.reshape(tbl_count * slot_count, half, count)


def exchange_line(code, codes, scales, shard_slot):
    nodes = code.nodes
    _, samples = codes.shape[1:]
    count = samples // (2 * nodes)
    me = lax.axis_index("tbl").astype(jnp.int32)
    table = plan(shard_slot, me[None], code)
    rounds = table[4, 0]

    def index(place, col):
        return place * 2 + col

    swaps = []
    for side in range(2):
        pairs = [(index(a, c), index(a + 1, c)) for a in range(side, nodes - 1, 2) for c in range(2)]
        swaps.append(pairs + [(b, a) for a, b in pairs])
    across = [(index(a, c), index(a, 1 - c)) for a in range(nodes) for c in range(2)]

    def piece(n, after):
        part = column_piece(nodes, n, me[None], codes, scales, after, count)
        return lax.ppermute(part, "tbl", across)

    def swap(sends):
        swapped = []
        for sent, pairs in zip(sends, swaps):
            swapped.append(lax.ppermute(sent, "tbl", pairs))
        return swapped

    def run(limit, open_end):
        return rounds_of(limit, open_end)

    def rounds_of(limit, open_end):
        pool, arrived, pieces = None, [], [piece(0, scales)]
        for r in range(limit):
            ready = [p for n, p in enumerate(pieces[:nodes - 1]) if PIECE_ROUND[n] <= r]
            recv = arrived[r - LAG] if r >= LAG else None
            pool, *sends = turn(code, table, r, codes, scales, ready, pool, recv, count)
            arrived.append(swap(sends))
            if r in PIECE_AFTER[1:]:
                pieces.append(piece(len(pieces), sends[0]))
        final, early, late = jnp.int32(limit), arrived[-2], arrived[-1]
        if open_end:
            pool, early, late, pieces = lax.optimization_barrier((pool, early, late, pieces))

            def step(state):
                r, pool, early, late = state
                pool, *sends = turn(code, table, r[None], codes, scales, pieces[:-1], pool, early, count)
                return r + 1, pool, late, swap(sends)

            final, pool, early, late = lax.while_loop(lambda state: state[0] < rounds, step, (final, pool, early, late))
        pool = settle(table, final[None] - 2, pool, early)
        return settle(table, final[None] - 1, pool, late), pieces[-1]

    steps = [functools.partial(run, limit, limit == ROUND_STEPS[-1]) for limit in ROUND_STEPS]
    choice = sum((rounds > limit).astype(jnp.int32) for limit in ROUND_STEPS[:-1])
    pool, piece_own = lax.switch(choice, steps)
    return table, pool, piece_own


def per_device(codes, scales, shard_slot, *parameters):
    layers = tuple(zip(parameters[0::2], parameters[1::2]))
    slots = codes.shape[0]
    tbl_count = lax.axis_size("tbl")
    shards = 2 * TABLES
    if tbl_count % 4 == 0 and slots >= tbl_count:
        code = Codes(tbl_count // 2, slots)
        places, pool, piece = exchange_line(code, codes, scales, shard_slot)
        limits = (slots, code.piece, code.pool, 5)
    else:
        pool = exchange_all(codes, scales)
        piece, places, limits = pool, shard_positions(shard_slot, shards)[None, :], (slots, 0, 0, 0)
    logits = score(pool, codes, piece, scales, places, shards, limits, layers)
    return lax.all_gather(logits, "pair", axis=0, tiled=True)


def solution(mesh):
    return jax.shard_map(
        per_device,
        mesh=mesh,
        in_specs=(P("tbl", None, "pair"), P("tbl", "pair")) + (P(),) * 11,
        out_specs=P(None, "tbl"),
        check_vma=False,
    )
```

profile of v0, /device:TPU:0, one launch (start us, length us, event | category | flops | bytes accessed | tf_op | source)
XLA Modules:
  0.0 201.1 jit_solution(8418312179790511159)
XLA Ops:
  0.0 1.1 plan.1.pos_ref
  3.2 174.9 %conditional.1 = (bf16[236,64,512]{2,1,0:T(8,128)(2,1)}, bf16[14,64,512]{2,1,0:T(8,128)(2,1)}) conditional(s32[]{:T(128)} %clamp.3, (s32[]{:T(128)}, bf16[14,64,4096]{2,1,0:T(8,128)(2,1)}, f32[14,4096]{1,0:T(8,128)}, s32[8,256]{1,0:T(8,128)S(1)}) %tuple.22, (s32[]{:T(128)}, bf16[14,64,4096]{2,1,0:T(8,128)(2,1)}, ...), branch_computations={%region_0.0_spmd, %region_1.0_spmd, %region_2.0_spmd} | conditional | flops 8126468 | bytes 159778672 | solution.py:549
  3.5 3.2 %piece.20 = bf16[14,64,512]{2,1,0:T(8,128)(2,1)S(1)} custom-call(s32[1]{0:T(128)} %bitcast.3.me_ref, bf16[14,64,4096]{2,1,0:T(8,128)(2,1)} %get-tuple-element.373.codes_ref.refs_0_, f32[14,4096]{1,0:T(8,128)} %get-tuple-element.374.scales_ref.after_ref.refs_1_, f32[14,4096]{1,0:T(8,128)} %get-tuple-element.374.scales_ref.after_ref.refs_1_), custom_call_target="tpu_custom_call" | custom-call | flops 458752 | bytes 1835008 | tf_op jit(solution)/shard_map/cond/branch_2_fun/piece/pallas_call | solution.py:305
  6.7 3.1 %collective-permute-start.60 = (bf16[14,64,512]{2,1,0:T(8,128)(2,1)S(1)}, bf16[14,64,512]{2,1,0:T(8,128)(2,1)S(1)}, u32[]{:S(2)}, u32[]{:S(2)}) collective-permute-start(bf16[14,64,512]{2,1,0:T(8,128)(2,1)S(1)} %piece.20), channel_id=1, source_target_pairs={{0,4},{4,0},{8,12},{12,8},{16,20},{20,16},{24,28},{28,24},{1,5},{5... | collective-permute-start | bytes 2752520 | tf_op jit(solution)/shard_map/cond/branch_2_fun/ppermute | solution.py:514
  9.8 3.6 %turn.66 = (bf16[236,64,512]{2,1,0:T(8,128)(2,1)}, bf16[6,64,512]{2,1,0:T(8,128)(2,1)S(1)}, bf16[6,64,512]{2,1,0:T(8,128)(2,1)S(1)}) custom-call(s32[8,256]{1,0:T(8,128)S(1)} %get-tuple-element.372.table_ref, bf16[14,64,4096]{2,1,0:T(8,128)(2,1)} %get-tuple-element.373.codes_ref.refs_0_, f32[14,4096]{1,0:T(8,128)} %get-tuple-element.374.scales_ref.after_ref.refs_1_), custom_call_target="tpu_custom_call" | custom-call | flops 393216 | bytes 3145728 | tf_op jit(solution)/shard_map/cond/branch_2_fun/turn/pallas_call | solution.py:261
  13.4 1.2 collective-permute-start.61
  14.6 0.7 collective-permute-start.62
  15.3 1.6 turn.67
  16.9 5.7 %collective-permute-start.64 = (bf16[6,64,512]{2,1,0:T(8,128)(2,1)S(1)}, bf16[6,64,512]{2,1,0:T(8,128)(2,1)S(1)}, u32[]{:S(2)}, u32[]{:S(2)}) collective-permute-start(bf16[6,64,512]{2,1,0:T(8,128)(2,1)S(1)} %get-tuple-element.194), channel_id=1, source_target_pairs={{0,8},{4,12},{16,24},{20,28},{8,0},{12,4},{24,16},{28,20},{1,9},{5... | collective-permute-start | bytes 1179656 | tf_op jit(solution)/shard_map/cond/branch_2_fun/ppermute | solution.py:519
  23.3 2.2 %collective-permute-done.61.refs_3_ = bf16[6,64,512]{2,1,0:T(8,128)(2,1)S(1)} collective-permute-done((bf16[6,64,512]{2,1,0:T(8,128)(2,1)S(1)}, bf16[6,64,512]{2,1,0:T(8,128)(2,1)S(1)}, u32[]{:S(2)}, u32[]{:S(2)}) %collective-permute-start.61) | collective-permute-done | bytes 393248 | tf_op jit(solution)/shard_map/cond/branch_2_fun/ppermute | solution.py:519
  25.4 2.5 %turn.68 = (bf16[236,64,512]{2,1,0:T(8,128)(2,1)}, bf16[6,64,512]{2,1,0:T(8,128)(2,1)S(1)}, bf16[6,64,512]{2,1,0:T(8,128)(2,1)S(1)}) custom-call(s32[8,256]{1,0:T(8,128)S(1)} %get-tuple-element.372.table_ref, bf16[14,64,4096]{2,1,0:T(8,128)(2,1)S(1)} %bitcast.26, f32[14,4096]{1,0:T(8,128)S(1)} %copy-done.11, ...), custom_call_target="tpu_custom_call", output_to_operand_aliasing={{0}: (3, {})} | custom-call | flops 393216 | bytes 3145728 | tf_op jit(solution)/shard_map/cond/branch_2_fun/turn/pallas_call | solution.py:261
  28.0 6.2 %collective-permute-start.66 = (bf16[6,64,512]{2,1,0:T(8,128)(2,1)S(1)}, bf16[6,64,512]{2,1,0:T(8,128)(2,1)S(1)}, u32[]{:S(2)}, u32[]{:S(2)}) collective-permute-start(bf16[6,64,512]{2,1,0:T(8,128)(2,1)S(1)} %get-tuple-element.192.after_ref), channel_id=1, source_target_pairs={{0,8},{4,12},{16,24},{20,28},{8,0},{12,4},{24,16},{28,20},{1,9},{5... | collective-permute-start | bytes 1179656 | tf_op jit(solution)/shard_map/cond/branch_2_fun/ppermute | solution.py:519
  34.6 0.7 collective-permute-start.67
  35.3 2.5 %turn.69 = (bf16[236,64,512]{2,1,0:T(8,128)(2,1)}, bf16[6,64,512]{2,1,0:T(8,128)(2,1)S(1)}, bf16[6,64,512]{2,1,0:T(8,128)(2,1)S(1)}) custom-call(s32[8,256]{1,0:T(8,128)S(1)} %get-tuple-element.372.table_ref, bf16[14,64,4096]{2,1,0:T(8,128)(2,1)S(1)} %bitcast.26, f32[14,4096]{1,0:T(8,128)S(1)} %copy-done.11, ...), custom_call_target="tpu_custom_call", output_to_operand_aliasing={{0}: (4, {})} | custom-call | flops 393216 | bytes 3145728 | tf_op jit(solution)/shard_map/cond/branch_2_fun/turn/pallas_call | solution.py:261
  37.8 4.3 %collective-permute-start.69 = (bf16[6,64,512]{2,1,0:T(8,128)(2,1)S(1)}, bf16[6,64,512]{2,1,0:T(8,128)(2,1)S(1)}, u32[]{:S(2)}, u32[]{:S(2)}) collective-permute-start(bf16[6,64,512]{2,1,0:T(8,128)(2,1)S(1)} %get-tuple-element.200), channel_id=1, source_target_pairs={{0,8},{4,12},{16,24},{20,28},{8,0},{12,4},{24,16},{28,20},{1,9},{5... | collective-permute-start | bytes 1179656 | tf_op jit(solution)/shard_map/cond/branch_2_fun/ppermute | solution.py:519
  42.2 2.5 %turn.70 = (bf16[236,64,512]{2,1,0:T(8,128)(2,1)}, bf16[6,64,512]{2,1,0:T(8,128)(2,1)S(1)}, bf16[6,64,512]{2,1,0:T(8,128)(2,1)S(1)}) custom-call(s32[8,256]{1,0:T(8,128)S(1)} %get-tuple-element.372.table_ref, bf16[14,64,4096]{2,1,0:T(8,128)(2,1)S(1)} %bitcast.26, f32[14,4096]{1,0:T(8,128)S(1)} %copy-done.11, ...), custom_call_target="tpu_custom_call", output_to_operand_aliasing={{0}: (4, {})} | custom-call | flops 393216 | bytes 3145728 | tf_op jit(solution)/shard_map/cond/branch_2_fun/turn/pallas_call | solution.py:261
  45.1 1.3 collective-permute-start.68
  47.0 7.4 %collective-permute-start.71 = (bf16[6,64,512]{2,1,0:T(8,128)(2,1)S(1)}, bf16[6,64,512]{2,1,0:T(8,128)(2,1)S(1)}, u32[]{:S(2)}, u32[]{:S(2)}) collective-permute-start(bf16[6,64,512]{2,1,0:T(8,128)(2,1)S(1)} %get-tuple-element.198.after_ref), channel_id=1, source_target_pairs={{0,8},{4,12},{16,24},{20,28},{8,0},{12,4},{24,16},{28,20},{1,9},{5... | collective-permute-start | bytes 1179656 | tf_op jit(solution)/shard_map/cond/branch_2_fun/ppermute | solution.py:519
  54.4 0.7 collective-permute-start.72
  55.1 2.7 %collective-permute-done.63.refs_3_ = bf16[14,64,512]{2,1,0:T(8,128)(2,1)S(1)} collective-permute-done((bf16[14,64,512]{2,1,0:T(8,128)(2,1)S(1)}, bf16[14,64,512]{2,1,0:T(8,128)(2,1)S(1)}, u32[]{:S(2)}, u32[]{:S(2)}) %collective-permute-start.63) | collective-permute-done | bytes 917536 | tf_op jit(solution)/shard_map/cond/branch_2_fun/ppermute | solution.py:514
  57.8 3.0 %turn.71 = (bf16[236,64,512]{2,1,0:T(8,128)(2,1)}, bf16[6,64,512]{2,1,0:T(8,128)(2,1)S(1)}, bf16[6,64,512]{2,1,0:T(8,128)(2,1)S(1)}) custom-call(s32[8,256]{1,0:T(8,128)S(1)} %get-tuple-element.372.table_ref, bf16[14,64,4096]{2,1,0:T(8,128)(2,1)S(1)} %bitcast.26, f32[14,4096]{1,0:T(8,128)S(1)} %copy-done.11, ...), custom_call_target="tpu_custom_call", output_to_operand_aliasing={{0}: (5, {})} | custom-call | flops 393216 | bytes 3145728 | tf_op jit(solution)/shard_map/cond/branch_2_fun/turn/pallas_call | solution.py:261
  60.8 6.5 %collective-permute-start.73 = (bf16[6,64,512]{2,1,0:T(8,128)(2,1)S(1)}, bf16[6,64,512]{2,1,0:T(8,128)(2,1)S(1)}, u32[]{:S(2)}, u32[]{:S(2)}) collective-permute-start(bf16[6,64,512]{2,1,0:T(8,128)(2,1)S(1)} %get-tuple-element.205), channel_id=1, source_target_pairs={{0,8},{4,12},{16,24},{20,28},{8,0},{12,4},{24,16},{28,20},{1,9},{5... | collective-permute-start | bytes 1179656 | tf_op jit(solution)/shard_map/cond/branch_2_fun/ppermute | solution.py:519
  67.3 0.7 collective-permute-start.74
  68.0 3.0 %turn.72 = (bf16[236,64,512]{2,1,0:T(8,128)(2,1)}, bf16[6,64,512]{2,1,0:T(8,128)(2,1)S(1)}, bf16[6,64,512]{2,1,0:T(8,128)(2,1)S(1)}) custom-call(s32[8,256]{1,0:T(8,128)S(1)} %get-tuple-element.372.table_ref, bf16[14,64,4096]{2,1,0:T(8,128)(2,1)S(1)} %bitcast.26, f32[14,4096]{1,0:T(8,128)S(1)} %copy-done.11, ...), custom_call_target="tpu_custom_call", output_to_operand_aliasing={{0}: (5, {})} | custom-call | flops 393216 | bytes 3145728 | tf_op jit(solution)/shard_map/cond/branch_2_fun/turn/pallas_call | solution.py:261
  71.1 4.7 %collective-permute-start.75 = (bf16[6,64,512]{2,1,0:T(8,128)(2,1)S(1)}, bf16[6,64,512]{2,1,0:T(8,128)(2,1)S(1)}, u32[]{:S(2)}, u32[]{:S(2)}) collective-permute-start(bf16[6,64,512]{2,1,0:T(8,128)(2,1)S(1)} %get-tuple-element.208.after_ref), channel_id=1, source_target_pairs={{0,8},{4,12},{16,24},{20,28},{8,0},{12,4},{24,16},{28,20},{1,9},{5... | collective-permute-start | bytes 1179656 | tf_op jit(solution)/shard_map/cond/branch_2_fun/ppermute | solution.py:519
  76.5 3.1 %turn.73 = (bf16[236,64,512]{2,1,0:T(8,128)(2,1)}, bf16[6,64,512]{2,1,0:T(8,128)(2,1)S(1)}, bf16[6,64,512]{2,1,0:T(8,128)(2,1)S(1)}) custom-call(s32[8,256]{1,0:T(8,128)S(1)} %get-tuple-element.372.table_ref, bf16[14,64,4096]{2,1,0:T(8,128)(2,1)S(1)} %bitcast.26, f32[14,4096]{1,0:T(8,128)S(1)} %copy-done.11, ...), custom_call_target="tpu_custom_call", output_to_operand_aliasing={{0}: (6, {})} | custom-call | flops 393216 | bytes 3145728 | tf_op jit(solution)/shard_map/cond/branch_2_fun/turn/pallas_call | solution.py:261
  79.6 5.4 %collective-permute-start.77 = (bf16[6,64,512]{2,1,0:T(8,128)(2,1)S(1)}, bf16[6,64,512]{2,1,0:T(8,128)(2,1)S(1)}, u32[]{:S(2)}, u32[]{:S(2)}) collective-permute-start(bf16[6,64,512]{2,1,0:T(8,128)(2,1)S(1)} %get-tuple-element.211), channel_id=1, source_target_pairs={{0,8},{4,12},{16,24},{20,28},{8,0},{12,4},{24,16},{28,20},{1,9},{5... | collective-permute-start | bytes 1179656 | tf_op jit(solution)/shard_map/cond/branch_2_fun/ppermute | solution.py:519
  85.7 3.1 %turn.74 = (bf16[236,64,512]{2,1,0:T(8,128)(2,1)}, bf16[6,64,512]{2,1,0:T(8,128)(2,1)S(1)}, bf16[6,64,512]{2,1,0:T(8,128)(2,1)S(1)}) custom-call(s32[8,256]{1,0:T(8,128)S(1)} %get-tuple-element.372.table_ref, bf16[14,64,4096]{2,1,0:T(8,128)(2,1)S(1)} %bitcast.26, f32[14,4096]{1,0:T(8,128)S(1)} %copy-done.11, ...), custom_call_target="tpu_custom_call", output_to_operand_aliasing={{0}: (6, {})} | custom-call | flops 393216 | bytes 3145728 | tf_op jit(solution)/shard_map/cond/branch_2_fun/turn/pallas_call | solution.py:261
  88.8 4.6 %collective-permute-start.79 = (bf16[6,64,512]{2,1,0:T(8,128)(2,1)S(1)}, bf16[6,64,512]{2,1,0:T(8,128)(2,1)S(1)}, u32[]{:S(2)}, u32[]{:S(2)}) collective-permute-start(bf16[6,64,512]{2,1,0:T(8,128)(2,1)S(1)} %get-tuple-element.214), channel_id=1, source_target_pairs={{0,8},{4,12},{16,24},{20,28},{8,0},{12,4},{24,16},{28,20},{1,9},{5... | collective-permute-start | bytes 1179656 | tf_op jit(solution)/shard_map/cond/branch_2_fun/ppermute | solution.py:519
  94.3 3.1 %turn.75 = (bf16[236,64,512]{2,1,0:T(8,128)(2,1)}, bf16[6,64,512]{2,1,0:T(8,128)(2,1)S(1)}, bf16[6,64,512]{2,1,0:T(8,128)(2,1)S(1)}) custom-call(s32[8,256]{1,0:T(8,128)S(1)} %get-tuple-element.372.table_ref, bf16[14,64,4096]{2,1,0:T(8,128)(2,1)S(1)} %bitcast.26, f32[14,4096]{1,0:T(8,128)S(1)} %copy-done.11, ...), custom_call_target="tpu_custom_call", output_to_operand_aliasing={{0}: (6, {})} | custom-call | flops 393216 | bytes 3145728 | tf_op jit(solution)/shard_map/cond/branch_2_fun/turn/pallas_call | solution.py:261
  97.4 4.6 %collective-permute-start.81 = (bf16[6,64,512]{2,1,0:T(8,128)(2,1)S(1)}, bf16[6,64,512]{2,1,0:T(8,128)(2,1)S(1)}, u32[]{:S(2)}, u32[]{:S(2)}) collective-permute-start(bf16[6,64,512]{2,1,0:T(8,128)(2,1)S(1)} %get-tuple-element.217), channel_id=1, source_target_pairs={{0,8},{4,12},{16,24},{20,28},{8,0},{12,4},{24,16},{28,20},{1,9},{5... | collective-permute-start | bytes 1179656 | tf_op jit(solution)/shard_map/cond/branch_2_fun/ppermute | solution.py:519
  102.0 0.7 collective-permute-start.82
  103.3 3.1 %turn.76 = (bf16[236,64,512]{2,1,0:T(8,128)(2,1)}, bf16[6,64,512]{2,1,0:T(8,128)(2,1)S(1)}, bf16[6,64,512]{2,1,0:T(8,128)(2,1)S(1)}) custom-call(s32[8,256]{1,0:T(8,128)S(1)} %get-tuple-element.372.table_ref, bf16[14,64,4096]{2,1,0:T(8,128)(2,1)S(1)} %bitcast.26, f32[14,4096]{1,0:T(8,128)S(1)} %copy-done.11, ...), custom_call_target="tpu_custom_call", output_to_operand_aliasing={{0}: (6, {})} | custom-call | flops 393216 | bytes 3145728 | tf_op jit(solution)/shard_map/cond/branch_2_fun/turn/pallas_call | solution.py:261
  106.4 3.9 %collective-permute-start.83 = (bf16[6,64,512]{2,1,0:T(8,128)(2,1)S(1)}, bf16[6,64,512]{2,1,0:T(8,128)(2,1)S(1)}, u32[]{:S(2)}, u32[]{:S(2)}) collective-permute-start(bf16[6,64,512]{2,1,0:T(8,128)(2,1)S(1)} %get-tuple-element.220), channel_id=1, source_target_pairs={{0,8},{4,12},{16,24},{20,28},{8,0},{12,4},{24,16},{28,20},{1,9},{5... | collective-permute-start | bytes 1179656 | tf_op jit(solution)/shard_map/cond/branch_2_fun/ppermute | solution.py:519
  110.3 0.7 collective-permute-start.84
  111.0 1.3 piece.23
  112.3 1.5 collective-permute-start.93
  113.9 3.1 %turn.77 = (bf16[236,64,512]{2,1,0:T(8,128)(2,1)}, bf16[6,64,512]{2,1,0:T(8,128)(2,1)S(1)}, bf16[6,64,512]{2,1,0:T(8,128)(2,1)S(1)}) custom-call(s32[8,256]{1,0:T(8,128)S(1)} %get-tuple-element.372.table_ref, bf16[14,64,4096]{2,1,0:T(8,128)(2,1)S(1)} %bitcast.26, f32[14,4096]{1,0:T(8,128)S(1)} %copy-done.11, ...), custom_call_target="tpu_custom_call", output_to_operand_aliasing={{0}: (6, {})} | custom-call | flops 393216 | bytes 3145728 | tf_op jit(solution)/shard_map/cond/branch_2_fun/turn/pallas_call | solution.py:261
  116.9 2.7 %collective-permute-start.85 = (bf16[6,64,512]{2,1,0:T(8,128)(2,1)S(1)}, bf16[6,64,512]{2,1,0:T(8,128)(2,1)S(1)}, u32[]{:S(2)}, u32[]{:S(2)}) collective-permute-start(bf16[6,64,512]{2,1,0:T(8,128)(2,1)S(1)} %get-tuple-element.223), channel_id=1, source_target_pairs={{0,8},{4,12},{16,24},{20,28},{8,0},{12,4},{24,16},{28,20},{1,9},{5... | collective-permute-start | bytes 1179656 | tf_op jit(solution)/shard_map/cond/branch_2_fun/ppermute | solution.py:519
  120.4 2.5 %turn.78 = (bf16[236,64,512]{2,1,0:T(8,128)(2,1)}, bf16[6,64,512]{2,1,0:T(8,128)(2,1)S(1)}, bf16[6,64,512]{2,1,0:T(8,128)(2,1)S(1)}) custom-call(s32[8,256]{1,0:T(8,128)S(1)} %get-tuple-element.372.table_ref, bf16[14,64,4096]{2,1,0:T(8,128)(2,1)S(1)} %bitcast.26, f32[14,4096]{1,0:T(8,128)S(1)} %copy-done.11, ...), custom_call_target="tpu_custom_call", output_to_operand_aliasing={{0}: (6, {})} | custom-call | flops 393216 | bytes 3145728 | tf_op jit(solution)/shard_map/cond/branch_2_fun/turn/pallas_call | solution.py:261
  122.9 4.4 %collective-permute-start.87 = (bf16[6,64,512]{2,1,0:T(8,128)(2,1)S(1)}, bf16[6,64,512]{2,1,0:T(8,128)(2,1)S(1)}, u32[]{:S(2)}, u32[]{:S(2)}) collective-permute-start(bf16[6,64,512]{2,1,0:T(8,128)(2,1)S(1)} %get-tuple-element.226), channel_id=1, source_target_pairs={{0,8},{4,12},{16,24},{20,28},{8,0},{12,4},{24,16},{28,20},{1,9},{5... | collective-permute-start | bytes 1179656 | tf_op jit(solution)/shard_map/cond/branch_2_fun/ppermute | solution.py:519
  128.0 3.4 %turn.79 = (bf16[236,64,512]{2,1,0:T(8,128)(2,1)}, bf16[6,64,512]{2,1,0:T(8,128)(2,1)}, bf16[6,64,512]{2,1,0:T(8,128)(2,1)}) custom-call(s32[8,256]{1,0:T(8,128)S(1)} %get-tuple-element.372.table_ref, bf16[14,64,4096]{2,1,0:T(8,128)(2,1)S(1)} %bitcast.26, f32[14,4096]{1,0:T(8,128)S(1)} %copy-done.11, ...), custom_call_target="tpu_custom_call", output_to_operand_aliasing={{0}: (6, {})} | custom-call | flops 393216 | bytes 3145728 | tf_op jit(solution)/shard_map/cond/branch_2_fun/turn/pallas_call | solution.py:261
  131.4 1.6 collective-permute-done.87.refs_6_
  133.1 3.5 %turn.80 = (bf16[236,64,512]{2,1,0:T(8,128)(2,1)}, bf16[6,64,512]{2,1,0:T(8,128)(2,1)}, bf16[6,64,512]{2,1,0:T(8,128)(2,1)}) custom-call(s32[8,256]{1,0:T(8,128)S(1)} %get-tuple-element.372.table_ref, bf16[14,64,4096]{2,1,0:T(8,128)(2,1)S(1)} %bitcast.26, f32[14,4096]{1,0:T(8,128)S(1)} %copy-done.11, ...), custom_call_target="tpu_custom_call", output_to_operand_aliasing={{0}: (6, {})} | custom-call | flops 393216 | bytes 3145728 | tf_op jit(solution)/shard_map/cond/branch_2_fun/turn/pallas_call | solution.py:261
  136.6 4.2 %collective-permute-start.91 = (bf16[6,64,512]{2,1,0:T(8,128)(2,1)}, bf16[6,64,512]{2,1,0:T(8,128)(2,1)}, u32[]{:S(2)}, u32[]{:S(2)}) collective-permute-start(bf16[6,64,512]{2,1,0:T(8,128)(2,1)} %get-tuple-element.231), channel_id=1, source_target_pairs={{0,8},{4,12},{16,24},{20,28},{8,0},{12,4},{24,16},{28,20},{1,9},{5... | collective-permute-start | bytes 1179656 | tf_op jit(solution)/shard_map/cond/branch_2_fun/ppermute | solution.py:519
  140.8 1.4 collective-permute-start.92
  142.2 2.1 %collective-permute-start.89 = (bf16[6,64,512]{2,1,0:T(8,128)(2,1)}, bf16[6,64,512]{2,1,0:T(8,128)(2,1)}, u32[]{:S(2)}, u32[]{:S(2)}) collective-permute-start(bf16[6,64,512]{2,1,0:T(8,128)(2,1)} %get-tuple-element.229), channel_id=1, source_target_pairs={{0,8},{4,12},{16,24},{20,28},{8,0},{12,4},{24,16},{28,20},{1,9},{5... | collective-permute-start | bytes 1179656 | tf_op jit(solution)/shard_map/cond/branch_2_fun/ppermute | solution.py:519
  144.3 1.4 collective-permute-start.90
  145.7 1.5 collective-permute-done.91
  147.2 4.2 %collective-permute-done.89 = bf16[6,64,512]{2,1,0:T(8,128)(2,1)} collective-permute-done((bf16[6,64,512]{2,1,0:T(8,128)(2,1)}, bf16[6,64,512]{2,1,0:T(8,128)(2,1)}, u32[]{:S(2)}, u32[]{:S(2)}) %collective-permute-start.89) | collective-permute-done | bytes 393248 | tf_op jit(solution)/shard_map/cond/branch_2_fun/ppermute | solution.py:519
  151.4 21.2 %while.17 = (s32[]{:T(128)}, bf16[236,64,512]{2,1,0:T(8,128)(2,1)}, bf16[6,64,512]{2,1,0:T(8,128)(2,1)}, bf16[6,64,512]{2,1,0:T(8,128)(2,1)}, bf16[6,64,512]{2,1...) while((s32[]{:T(128)}, bf16[236,64,512]{2,1,0:T(8,128)(2,1)}, ...), condition=%wide.region_4.0_spmd, body=%wide.region_3.0_spmd.sunk | while | flops 393218 | bytes 9437397 | solution.py:543
  152.2 6.0 %turn.81 = (bf16[236,64,512]{2,1,0:T(8,128)(2,1)}, bf16[6,64,512]{2,1,0:T(8,128)(2,1)}, bf16[6,64,512]{2,1,0:T(8,128)(2,1)}) custom-call(s32[8,256]{1,0:T(8,128)S(1)} %get-tuple-element.400.table_ref, s32[1]{0:T(128)} %bitcast.17.refs_0_, bf16[14,64,4096]{2,1,0:T(8,128)(2,1)} %get-tuple-element.401.refs_1_, ...), custom_call_target="tpu_custom_call", output_to_operand_aliasing={{0}: (7, {})} | custom-call | flops 393216 | bytes 3145728 | tf_op jit(solution)/shard_map/cond/branch_2_fun/while/body/turn/pallas_call | solution.py:261
  158.1 4.2 %collective-permute-start.58 = (bf16[6,64,512]{2,1,0:T(8,128)(2,1)}, bf16[6,64,512]{2,1,0:T(8,128)(2,1)}, u32[]{:S(2)}, u32[]{:S(2)}) collective-permute-start(bf16[6,64,512]{2,1,0:T(8,128)(2,1)} %get-tuple-element.363), channel_id=1, source_target_pairs={{0,8},{4,12},{16,24},{20,28},{8,0},{12,4},{24,16},{28,20},{1,9},{5... | collective-permute-start | bytes 1179656 | tf_op jit(solution)/shard_map/cond/branch_2_fun/while/body/ppermute | solution.py:519
  162.3 1.4 collective-permute-start.59
  163.7 1.8 copy.117
  165.5 1.8 copy.118
  167.3 1.1 collective-permute-done.58
  168.4 1.8 copy.119
  170.2 1.8 copy.120
  172.7 2.6 %settle.10.pool_in = bf16[236,64,512]{2,1,0:T(8,128)(2,1)} custom-call(s32[8,256]{1,0:T(8,128)S(1)} %get-tuple-element.586, s32[1]{0:T(128)} %bitcast.5.round_ref, bf16[236,64,512]{2,1,0:T(8,128)(2,1)} %get-tuple-element.243.pool_in, bf16[6,64,512]{2,1,0:T(8,128)(2,1)} %get-tuple-element.244.recv_a, ...), custom_call_target="tpu_custom_call", output_to_operand_aliasing={{}: (2, {})} | custom-call | tf_op jit(solution)/shard_map/cond/branch_2_fun/settle/pallas_call | solution.py:339
  175.3 2.6 %settle.11 = bf16[236,64,512]{2,1,0:T(8,128)(2,1)} custom-call(s32[8,256]{1,0:T(8,128)S(1)} %get-tuple-element.586, s32[1]{0:T(128)} %bitcast.4.round_ref, bf16[236,64,512]{2,1,0:T(8,128)(2,1)} %settle.10.pool_in, bf16[6,64,512]{2,1,0:T(8,128)(2,1)} %get-tuple-element.246.recv_a, ...), custom_call_target="tpu_custom_call", output_to_operand_aliasing={{}: (2, {})} | custom-call | tf_op jit(solution)/shard_map/cond/branch_2_fun/settle/pallas_call | solution.py:339
  178.9 1.1 copy-done.2
  180.0 15.3 %score.1 = f32[1,512]{1,0:T(1,128)S(1)} custom-call(s32[8,256]{1,0:T(8,128)S(1)} %plan.1.pos_ref, bf16[236,64,512]{2,1,0:T(8,128)(2,1)} %get-tuple-element.251.pool_ref, bf16[14,64,4096]{2,1,0:T(8,128)(2,1)} %codes_ref.1, bf16[14,64,512]{2,1,0:T(8,128)(2,1)} %get-tuple-element.252.piece_ref, f32[14,4096]{1,0:T(8,128)} %scales_ref.1, ...), custom_call_target="tpu_custom_call" | custom-call | flops 2112880640 | bytes 3538944 | tf_op jit(solution)/shard_map/score/pallas_call | solution.py:455
  195.3 5.2 %all-gather = f32[4,1,512]{2,1,0:T(1,128)S(1)} all-gather(f32[1,1,512]{2,1,0:T(1,128)S(1)} %bitcast.18), channel_id=1, replica_groups=mesh['tbl'=8,'pair'=4] {'pair'}, dimensions={0}, use_global_device_ids=true | all-gather | bytes 10240 | tf_op jit(solution)/shard_map/all_gather | solution.py:566
  (73 shorter events, 7.8 us)
Async XLA Ops:
  3.1 175.0 %copy-start.15 = (bf16[256]{0:T(256)(128)(2,1)S(1)}, bf16[256]{0:T(256)(128)(2,1)}, u32[]{:S(2)}) copy-start(bf16[256]{0:T(256)(128)(2,1)} %param.29) | copy-start | bytes 1540
  3.2 175.6 %copy-start = (bf16[1024,1024]{1,0:T(8,128)(2,1)S(1)}, bf16[1024,1024]{1,0:T(8,128)(2,1)}, u32[]{:S(2)}) copy-start(bf16[1024,1024]{1,0:T(8,128)(2,1)} %refs_1_.1) | copy-start | bytes 6291460
  3.2 175.6 %copy-start.1 = (bf16[1024,512]{1,0:T(8,128)(2,1)S(1)}, bf16[1024,512]{1,0:T(8,128)(2,1)}, u32[]{:S(2)}) copy-start(bf16[1024,512]{1,0:T(8,128)(2,1)} %refs_2_.1) | copy-start | bytes 3145732
  3.2 175.6 %copy-start.3 = (bf16[512,256]{1,0:T(8,128)(2,1)S(1)}, bf16[512,256]{1,0:T(8,128)(2,1)}, u32[]{:S(2)}) copy-start(bf16[512,256]{1,0:T(8,128)(2,1)} %refs_3_.1) | copy-start | bytes 786436
  3.2 175.6 %copy-start.4 = (f32[1024]{0:T(1024)S(1)}, f32[1024]{0:T(1024)}, u32[]{:S(2)}) copy-start(f32[1024]{0:T(1024)} %param.22) | copy-start | bytes 12292
  3.2 175.6 %copy-start.5 = (f32[1024]{0:T(1024)S(1)}, f32[1024]{0:T(1024)}, u32[]{:S(2)}) copy-start(f32[1024]{0:T(1024)} %param.24) | copy-start | bytes 12292
  3.2 175.6 %copy-start.6 = (f32[512]{0:T(512)S(1)}, f32[512]{0:T(512)}, u32[]{:S(2)}) copy-start(f32[512]{0:T(512)} %param.26) | copy-start | bytes 6148
  3.2 175.6 %copy-start.7 = (f32[256]{0:T(256)S(1)}, f32[256]{0:T(256)}, u32[]{:S(2)}) copy-start(f32[256]{0:T(256)} %param.28) | copy-start | bytes 3076
  3.5 11.8 %slice-start.2 = ((s8[7340032]{0:T(1024)(128)(4,1)}), s8[4194304]{0:T(1024)(128)(4,1)S(1)}, s32[]{:S(2)}) async-start(s8[7340032]{0:T(1024)(128)(4,1)} %bitcast.25), calls=%async_computation.2 | async-start | bytes 8388608 | tf_op jit(solution)/shard_map/cond
  3.5 11.8 %copy-start.11 = (f32[14,4096]{1,0:T(8,128)S(1)}, f32[14,4096]{1,0:T(8,128)}, u32[]{:S(2)}) copy-start(f32[14,4096]{1,0:T(8,128)} %get-tuple-element.374.scales_ref.after_ref.refs_1_) | copy-start | bytes 688132 | tf_op jit(solution)/shard_map/cond
  3.5 11.8 %slice-start.3 = ((s8[7340032]{0:T(1024)(128)(4,1)}), s8[3145728]{0:T(1024)(128)(4,1)S(1)}, s32[]{:S(2)}) async-start(s8[7340032]{0:T(1024)(128)(4,1)} %bitcast.25), calls=%async_computation.3 | async-start | bytes 6291456 | tf_op jit(solution)/shard_map/cond
  6.7 28.6 %collective-permute-start.60 = (bf16[14,64,512]{2,1,0:T(8,128)(2,1)S(1)}, bf16[14,64,512]{2,1,0:T(8,128)(2,1)S(1)}, u32[]{:S(2)}, u32[]{:S(2)}) collective-permute-start(bf16[14,64,512]{2,1,0:T(8,128)(2,1)S(1)} %piece.20), channel_id=1, source_target_pairs={{0,4},{4,0},{8,12},{12,8},{16,20},{20,16},{24,28},{28,24},{1,5},{5... | collective-permute-start | bytes 2752520 | tf_op jit(solution)/shard_map/cond/branch_2_fun/ppermute | solution.py:514
  13.4 12.1 %collective-permute-start.61 = (bf16[6,64,512]{2,1,0:T(8,128)(2,1)S(1)}, bf16[6,64,512]{2,1,0:T(8,128)(2,1)S(1)}, u32[]{:S(2)}, u32[]{:S(2)}) collective-permute-start(bf16[6,64,512]{2,1,0:T(8,128)(2,1)S(1)} %get-tuple-element.190), channel_id=1, source_target_pairs={{0,8},{4,12},{16,24},{20,28},{8,0},{12,4},{24,16},{28,20},{1,9},{5... | collective-permute-start | bytes 1179656 | tf_op jit(solution)/shard_map/cond/branch_2_fun/ppermute | solution.py:519
  14.6 10.8 %collective-permute-start.62 = (bf16[6,64,512]{2,1,0:T(8,128)(2,1)S(1)}, bf16[6,64,512]{2,1,0:T(8,128)(2,1)S(1)}, u32[]{:S(2)}, u32[]{:S(2)}) collective-permute-start(bf16[6,64,512]{2,1,0:T(8,128)(2,1)S(1)} %get-tuple-element.191), channel_id=1, source_target_pairs={{8,16},{12,20},{16,8},{20,12},{9,17},{13,21},{17,9},{21,13},{10,18... | collective-permute-start | bytes 1179656 | tf_op jit(solution)/shard_map/cond/branch_2_fun/ppermute | solution.py:519
  16.9 17.7 %collective-permute-start.64 = (bf16[6,64,512]{2,1,0:T(8,128)(2,1)S(1)}, bf16[6,64,512]{2,1,0:T(8,128)(2,1)S(1)}, u32[]{:S(2)}, u32[]{:S(2)}) collective-permute-start(bf16[6,64,512]{2,1,0:T(8,128)(2,1)S(1)} %get-tuple-element.194), channel_id=1, source_target_pairs={{0,8},{4,12},{16,24},{20,28},{8,0},{12,4},{24,16},{28,20},{1,9},{5... | collective-permute-start | bytes 1179656 | tf_op jit(solution)/shard_map/cond/branch_2_fun/ppermute | solution.py:519
  22.6 12.7 %collective-permute-start.65 = (bf16[6,64,512]{2,1,0:T(8,128)(2,1)S(1)}, bf16[6,64,512]{2,1,0:T(8,128)(2,1)S(1)}, u32[]{:S(2)}, u32[]{:S(2)}) collective-permute-start(bf16[6,64,512]{2,1,0:T(8,128)(2,1)S(1)} %get-tuple-element.195), channel_id=1, source_target_pairs={{8,16},{12,20},{16,8},{20,12},{9,17},{13,21},{17,9},{21,13},{10,18... | collective-permute-start | bytes 1179656 | tf_op jit(solution)/shard_map/cond/branch_2_fun/ppermute | solution.py:519
  28.0 14.2 %collective-permute-start.66 = (bf16[6,64,512]{2,1,0:T(8,128)(2,1)S(1)}, bf16[6,64,512]{2,1,0:T(8,128)(2,1)S(1)}, u32[]{:S(2)}, u32[]{:S(2)}) collective-permute-start(bf16[6,64,512]{2,1,0:T(8,128)(2,1)S(1)} %get-tuple-element.192.after_ref), channel_id=1, source_target_pairs={{0,8},{4,12},{16,24},{20,28},{8,0},{12,4},{24,16},{28,20},{1,9},{5... | collective-permute-start | bytes 1179656 | tf_op jit(solution)/shard_map/cond/branch_2_fun/ppermute | solution.py:519
  34.5 23.3 %collective-permute-start.63 = (bf16[14,64,512]{2,1,0:T(8,128)(2,1)S(1)}, bf16[14,64,512]{2,1,0:T(8,128)(2,1)S(1)}, u32[]{:S(2)}, u32[]{:S(2)}) collective-permute-start(bf16[14,64,512]{2,1,0:T(8,128)(2,1)S(1)} %piece.21), channel_id=1, source_target_pairs={{0,4},{4,0},{8,12},{12,8},{16,20},{20,16},{24,28},{28,24},{1,5},{5... | collective-permute-start | bytes 2752520 | tf_op jit(solution)/shard_map/cond/branch_2_fun/ppermute | solution.py:514
  34.6 7.6 %collective-permute-start.67 = (bf16[6,64,512]{2,1,0:T(8,128)(2,1)S(1)}, bf16[6,64,512]{2,1,0:T(8,128)(2,1)S(1)}, u32[]{:S(2)}, u32[]{:S(2)}) collective-permute-start(bf16[6,64,512]{2,1,0:T(8,128)(2,1)S(1)} %get-tuple-element.197), channel_id=1, source_target_pairs={{8,16},{12,20},{16,8},{20,12},{9,17},{13,21},{17,9},{21,13},{10,18... | collective-permute-start | bytes 1179656 | tf_op jit(solution)/shard_map/cond/branch_2_fun/ppermute | solution.py:519
  35.3 97.7 %copy-start.12 = (bf16[14,64,512]{2,1,0:T(8,128)(2,1)}, bf16[14,64,512]{2,1,0:T(8,128)(2,1)S(1)}, u32[]{:S(2)}) copy-start(bf16[14,64,512]{2,1,0:T(8,128)(2,1)S(1)} %collective-permute-done.60.refs_2_) | copy-start | bytes 2752516 | tf_op jit(solution)/shard_map/cond
  37.8 16.6 %collective-permute-start.69 = (bf16[6,64,512]{2,1,0:T(8,128)(2,1)S(1)}, bf16[6,64,512]{2,1,0:T(8,128)(2,1)S(1)}, u32[]{:S(2)}, u32[]{:S(2)}) collective-permute-start(bf16[6,64,512]{2,1,0:T(8,128)(2,1)S(1)} %get-tuple-element.200), channel_id=1, source_target_pairs={{0,8},{4,12},{16,24},{20,28},{8,0},{12,4},{24,16},{28,20},{1,9},{5... | collective-permute-start | bytes 1179656 | tf_op jit(solution)/shard_map/cond/branch_2_fun/ppermute | solution.py:519
  45.1 31.4 %collective-permute-start.68 = (bf16[14,64,512]{2,1,0:T(8,128)(2,1)S(1)}, bf16[14,64,512]{2,1,0:T(8,128)(2,1)S(1)}, u32[]{:S(2)}, u32[]{:S(2)}) collective-permute-start(bf16[14,64,512]{2,1,0:T(8,128)(2,1)S(1)} %piece.22), channel_id=1, source_target_pairs={{0,4},{4,0},{8,12},{12,8},{16,20},{20,16},{24,28},{28,24},{1,5},{5... | collective-permute-start | bytes 2752520 | tf_op jit(solution)/shard_map/cond/branch_2_fun/ppermute | solution.py:514
  46.4 8.8 %collective-permute-start.70 = (bf16[6,64,512]{2,1,0:T(8,128)(2,1)S(1)}, bf16[6,64,512]{2,1,0:T(8,128)(2,1)S(1)}, u32[]{:S(2)}, u32[]{:S(2)}) collective-permute-start(bf16[6,64,512]{2,1,0:T(8,128)(2,1)S(1)} %get-tuple-element.201), channel_id=1, source_target_pairs={{8,16},{12,20},{16,8},{20,12},{9,17},{13,21},{17,9},{21,13},{10,18... | collective-permute-start | bytes 1179656 | tf_op jit(solution)/shard_map/cond/branch_2_fun/ppermute | solution.py:519
  47.0 21.0 %collective-permute-start.71 = (bf16[6,64,512]{2,1,0:T(8,128)(2,1)S(1)}, bf16[6,64,512]{2,1,0:T(8,128)(2,1)S(1)}, u32[]{:S(2)}, u32[]{:S(2)}) collective-permute-start(bf16[6,64,512]{2,1,0:T(8,128)(2,1)S(1)} %get-tuple-element.198.after_ref), channel_id=1, source_target_pairs={{0,8},{4,12},{16,24},{20,28},{8,0},{12,4},{24,16},{28,20},{1,9},{5... | collective-permute-start | bytes 1179656 | tf_op jit(solution)/shard_map/cond/branch_2_fun/ppermute | solution.py:519
  54.4 13.6 %collective-permute-start.72 = (bf16[6,64,512]{2,1,0:T(8,128)(2,1)S(1)}, bf16[6,64,512]{2,1,0:T(8,128)(2,1)S(1)}, u32[]{:S(2)}, u32[]{:S(2)}) collective-permute-start(bf16[6,64,512]{2,1,0:T(8,128)(2,1)S(1)} %get-tuple-element.203), channel_id=1, source_target_pairs={{8,16},{12,20},{16,8},{20,12},{9,17},{13,21},{17,9},{21,13},{10,18... | collective-permute-start | bytes 1179656 | tf_op jit(solution)/shard_map/cond/branch_2_fun/ppermute | solution.py:519
  57.8 75.3 %copy-start.13 = (bf16[14,64,512]{2,1,0:T(8,128)(2,1)}, bf16[14,64,512]{2,1,0:T(8,128)(2,1)S(1)}, u32[]{:S(2)}) copy-start(bf16[14,64,512]{2,1,0:T(8,128)(2,1)S(1)} %collective-permute-done.63.refs_3_) | copy-start | bytes 2752516 | tf_op jit(solution)/shard_map/cond
  60.8 15.6 %collective-permute-start.73 = (bf16[6,64,512]{2,1,0:T(8,128)(2,1)S(1)}, bf16[6,64,512]{2,1,0:T(8,128)(2,1)S(1)}, u32[]{:S(2)}, u32[]{:S(2)}) collective-permute-start(bf16[6,64,512]{2,1,0:T(8,128)(2,1)S(1)} %get-tuple-element.205), channel_id=1, source_target_pairs={{0,8},{4,12},{16,24},{20,28},{8,0},{12,4},{24,16},{28,20},{1,9},{5... | collective-permute-start | bytes 1179656 | tf_op jit(solution)/shard_map/cond/branch_2_fun/ppermute | solution.py:519
  67.3 9.1 %collective-permute-start.74 = (bf16[6,64,512]{2,1,0:T(8,128)(2,1)S(1)}, bf16[6,64,512]{2,1,0:T(8,128)(2,1)S(1)}, u32[]{:S(2)}, u32[]{:S(2)}) collective-permute-start(bf16[6,64,512]{2,1,0:T(8,128)(2,1)S(1)} %get-tuple-element.206), channel_id=1, source_target_pairs={{8,16},{12,20},{16,8},{20,12},{9,17},{13,21},{17,9},{21,13},{10,18... | collective-permute-start | bytes 1179656 | tf_op jit(solution)/shard_map/cond/branch_2_fun/ppermute | solution.py:519
  71.1 14.6 %collective-permute-start.75 = (bf16[6,64,512]{2,1,0:T(8,128)(2,1)S(1)}, bf16[6,64,512]{2,1,0:T(8,128)(2,1)S(1)}, u32[]{:S(2)}, u32[]{:S(2)}) collective-permute-start(bf16[6,64,512]{2,1,0:T(8,128)(2,1)S(1)} %get-tuple-element.208.after_ref), channel_id=1, source_target_pairs={{0,8},{4,12},{16,24},{20,28},{8,0},{12,4},{24,16},{28,20},{1,9},{5... | collective-permute-start | bytes 1179656 | tf_op jit(solution)/shard_map/cond/branch_2_fun/ppermute | solution.py:519
  75.8 9.9 %collective-permute-start.76 = (bf16[6,64,512]{2,1,0:T(8,128)(2,1)S(1)}, bf16[6,64,512]{2,1,0:T(8,128)(2,1)S(1)}, u32[]{:S(2)}, u32[]{:S(2)}) collective-permute-start(bf16[6,64,512]{2,1,0:T(8,128)(2,1)S(1)} %get-tuple-element.209), channel_id=1, source_target_pairs={{8,16},{12,20},{16,8},{20,12},{9,17},{13,21},{17,9},{21,13},{10,18... | collective-permute-start | bytes 1179656 | tf_op jit(solution)/shard_map/cond/branch_2_fun/ppermute | solution.py:519
  76.5 56.6 %copy-start.14 = (bf16[14,64,512]{2,1,0:T(8,128)(2,1)}, bf16[14,64,512]{2,1,0:T(8,128)(2,1)S(1)}, u32[]{:S(2)}) copy-start(bf16[14,64,512]{2,1,0:T(8,128)(2,1)S(1)} %collective-permute-done.68.refs_4_) | copy-start | bytes 2752516 | tf_op jit(solution)/shard_map/cond
  79.6 14.7 %collective-permute-start.77 = (bf16[6,64,512]{2,1,0:T(8,128)(2,1)S(1)}, bf16[6,64,512]{2,1,0:T(8,128)(2,1)S(1)}, u32[]{:S(2)}, u32[]{:S(2)}) collective-permute-start(bf16[6,64,512]{2,1,0:T(8,128)(2,1)S(1)} %get-tuple-element.211), channel_id=1, source_target_pairs={{0,8},{4,12},{16,24},{20,28},{8,0},{12,4},{24,16},{28,20},{1,9},{5... | collective-permute-start | bytes 1179656 | tf_op jit(solution)/shard_map/cond/branch_2_fun/ppermute | solution.py:519
  85.0 9.3 %collective-permute-start.78 = (bf16[6,64,512]{2,1,0:T(8,128)(2,1)S(1)}, bf16[6,64,512]{2,1,0:T(8,128)(2,1)S(1)}, u32[]{:S(2)}, u32[]{:S(2)}) collective-permute-start(bf16[6,64,512]{2,1,0:T(8,128)(2,1)S(1)} %get-tuple-element.212), channel_id=1, source_target_pairs={{8,16},{12,20},{16,8},{20,12},{9,17},{13,21},{17,9},{21,13},{10,18... | collective-permute-start | bytes 1179656 | tf_op jit(solution)/shard_map/cond/branch_2_fun/ppermute | solution.py:519
  88.8 14.5 %collective-permute-start.79 = (bf16[6,64,512]{2,1,0:T(8,128)(2,1)S(1)}, bf16[6,64,512]{2,1,0:T(8,128)(2,1)S(1)}, u32[]{:S(2)}, u32[]{:S(2)}) collective-permute-start(bf16[6,64,512]{2,1,0:T(8,128)(2,1)S(1)} %get-tuple-element.214), channel_id=1, source_target_pairs={{0,8},{4,12},{16,24},{20,28},{8,0},{12,4},{24,16},{28,20},{1,9},{5... | collective-permute-start | bytes 1179656 | tf_op jit(solution)/shard_map/cond/branch_2_fun/ppermute | solution.py:519
  93.3 10.0 %collective-permute-start.80 = (bf16[6,64,512]{2,1,0:T(8,128)(2,1)S(1)}, bf16[6,64,512]{2,1,0:T(8,128)(2,1)S(1)}, u32[]{:S(2)}, u32[]{:S(2)}) collective-permute-start(bf16[6,64,512]{2,1,0:T(8,128)(2,1)S(1)} %get-tuple-element.215), channel_id=1, source_target_pairs={{8,16},{12,20},{16,8},{20,12},{9,17},{13,21},{17,9},{21,13},{10,18... | collective-permute-start | bytes 1179656 | tf_op jit(solution)/shard_map/cond/branch_2_fun/ppermute | solution.py:519
  97.4 16.5 %collective-permute-start.81 = (bf16[6,64,512]{2,1,0:T(8,128)(2,1)S(1)}, bf16[6,64,512]{2,1,0:T(8,128)(2,1)S(1)}, u32[]{:S(2)}, u32[]{:S(2)}) collective-permute-start(bf16[6,64,512]{2,1,0:T(8,128)(2,1)S(1)} %get-tuple-element.217), channel_id=1, source_target_pairs={{0,8},{4,12},{16,24},{20,28},{8,0},{12,4},{24,16},{28,20},{1,9},{5... | collective-permute-start | bytes 1179656 | tf_op jit(solution)/shard_map/cond/branch_2_fun/ppermute | solution.py:519
  102.0 11.9 %collective-permute-start.82 = (bf16[6,64,512]{2,1,0:T(8,128)(2,1)S(1)}, bf16[6,64,512]{2,1,0:T(8,128)(2,1)S(1)}, u32[]{:S(2)}, u32[]{:S(2)}) collective-permute-start(bf16[6,64,512]{2,1,0:T(8,128)(2,1)S(1)} %get-tuple-element.218), channel_id=1, source_target_pairs={{8,16},{12,20},{16,8},{20,12},{9,17},{13,21},{17,9},{21,13},{10,18... | collective-permute-start | bytes 1179656 | tf_op jit(solution)/shard_map/cond/branch_2_fun/ppermute | solution.py:519
  106.4 14.0 %collective-permute-start.83 = (bf16[6,64,512]{2,1,0:T(8,128)(2,1)S(1)}, bf16[6,64,512]{2,1,0:T(8,128)(2,1)S(1)}, u32[]{:S(2)}, u32[]{:S(2)}) collective-permute-start(bf16[6,64,512]{2,1,0:T(8,128)(2,1)S(1)} %get-tuple-element.220), channel_id=1, source_target_pairs={{0,8},{4,12},{16,24},{20,28},{8,0},{12,4},{24,16},{28,20},{1,9},{5... | collective-permute-start | bytes 1179656 | tf_op jit(solution)/shard_map/cond/branch_2_fun/ppermute | solution.py:519
  110.3 10.0 %collective-permute-start.84 = (bf16[6,64,512]{2,1,0:T(8,128)(2,1)S(1)}, bf16[6,64,512]{2,1,0:T(8,128)(2,1)S(1)}, u32[]{:S(2)}, u32[]{:S(2)}) collective-permute-start(bf16[6,64,512]{2,1,0:T(8,128)(2,1)S(1)} %get-tuple-element.221), channel_id=1, source_target_pairs={{8,16},{12,20},{16,8},{20,12},{9,17},{13,21},{17,9},{21,13},{10,18... | collective-permute-start | bytes 1179656 | tf_op jit(solution)/shard_map/cond/branch_2_fun/ppermute | solution.py:519
  112.3 33.4 %collective-permute-start.93 = (bf16[14,64,512]{2,1,0:T(8,128)(2,1)}, bf16[14,64,512]{2,1,0:T(8,128)(2,1)}, u32[]{:S(2)}, u32[]{:S(2)}) collective-permute-start(bf16[14,64,512]{2,1,0:T(8,128)(2,1)} %piece.23), channel_id=1, source_target_pairs={{0,4},{4,0},{8,12},{12,8},{16,20},{20,16},{24,28},{28,24},{1,5},{5... | collective-permute-start | bytes 2752520 | tf_op jit(solution)/shard_map/cond/branch_2_fun/ppermute | solution.py:514
  116.9 11.0 %collective-permute-start.85 = (bf16[6,64,512]{2,1,0:T(8,128)(2,1)S(1)}, bf16[6,64,512]{2,1,0:T(8,128)(2,1)S(1)}, u32[]{:S(2)}, u32[]{:S(2)}) collective-permute-start(bf16[6,64,512]{2,1,0:T(8,128)(2,1)S(1)} %get-tuple-element.223), channel_id=1, source_target_pairs={{0,8},{4,12},{16,24},{20,28},{8,0},{12,4},{24,16},{28,20},{1,9},{5... | collective-permute-start | bytes 1179656 | tf_op jit(solution)/shard_map/cond/branch_2_fun/ppermute | solution.py:519
  119.7 8.3 %collective-permute-start.86 = (bf16[6,64,512]{2,1,0:T(8,128)(2,1)S(1)}, bf16[6,64,512]{2,1,0:T(8,128)(2,1)S(1)}, u32[]{:S(2)}, u32[]{:S(2)}) collective-permute-start(bf16[6,64,512]{2,1,0:T(8,128)(2,1)S(1)} %get-tuple-element.224), channel_id=1, source_target_pairs={{8,16},{12,20},{16,8},{20,12},{9,17},{13,21},{17,9},{21,13},{10,18... | collective-permute-start | bytes 1179656 | tf_op jit(solution)/shard_map/cond/branch_2_fun/ppermute | solution.py:519
  122.9 10.1 %collective-permute-start.87 = (bf16[6,64,512]{2,1,0:T(8,128)(2,1)S(1)}, bf16[6,64,512]{2,1,0:T(8,128)(2,1)S(1)}, u32[]{:S(2)}, u32[]{:S(2)}) collective-permute-start(bf16[6,64,512]{2,1,0:T(8,128)(2,1)S(1)} %get-tuple-element.226), channel_id=1, source_target_pairs={{0,8},{4,12},{16,24},{20,28},{8,0},{12,4},{24,16},{28,20},{1,9},{5... | collective-permute-start | bytes 1179656 | tf_op jit(solution)/shard_map/cond/branch_2_fun/ppermute | solution.py:519
  127.3 5.8 %collective-permute-start.88 = (bf16[6,64,512]{2,1,0:T(8,128)(2,1)S(1)}, bf16[6,64,512]{2,1,0:T(8,128)(2,1)S(1)}, u32[]{:S(2)}, u32[]{:S(2)}) collective-permute-start(bf16[6,64,512]{2,1,0:T(8,128)(2,1)S(1)} %get-tuple-element.227), channel_id=1, source_target_pairs={{8,16},{12,20},{16,8},{20,12},{9,17},{13,21},{17,9},{21,13},{10,18... | collective-permute-start | bytes 1179656 | tf_op jit(solution)/shard_map/cond/branch_2_fun/ppermute | solution.py:519
  136.6 10.7 %collective-permute-start.91 = (bf16[6,64,512]{2,1,0:T(8,128)(2,1)}, bf16[6,64,512]{2,1,0:T(8,128)(2,1)}, u32[]{:S(2)}, u32[]{:S(2)}) collective-permute-start(bf16[6,64,512]{2,1,0:T(8,128)(2,1)} %get-tuple-element.231), channel_id=1, source_target_pairs={{0,8},{4,12},{16,24},{20,28},{8,0},{12,4},{24,16},{28,20},{1,9},{5... | collective-permute-start | bytes 1179656 | tf_op jit(solution)/shard_map/cond/branch_2_fun/ppermute | solution.py:519
  140.8 6.4 %collective-permute-start.92 = (bf16[6,64,512]{2,1,0:T(8,128)(2,1)}, bf16[6,64,512]{2,1,0:T(8,128)(2,1)}, u32[]{:S(2)}, u32[]{:S(2)}) collective-permute-start(bf16[6,64,512]{2,1,0:T(8,128)(2,1)} %get-tuple-element.232), channel_id=1, source_target_pairs={{8,16},{12,20},{16,8},{20,12},{9,17},{13,21},{17,9},{21,13},{10,18... | collective-permute-start | bytes 1179656 | tf_op jit(solution)/shard_map/cond/branch_2_fun/ppermute | solution.py:519
  142.2 9.2 %collective-permute-start.89 = (bf16[6,64,512]{2,1,0:T(8,128)(2,1)}, bf16[6,64,512]{2,1,0:T(8,128)(2,1)}, u32[]{:S(2)}, u32[]{:S(2)}) collective-permute-start(bf16[6,64,512]{2,1,0:T(8,128)(2,1)} %get-tuple-element.229), channel_id=1, source_target_pairs={{0,8},{4,12},{16,24},{20,28},{8,0},{12,4},{24,16},{28,20},{1,9},{5... | collective-permute-start | bytes 1179656 | tf_op jit(solution)/shard_map/cond/branch_2_fun/ppermute | solution.py:519
  144.3 7.2 %collective-permute-start.90 = (bf16[6,64,512]{2,1,0:T(8,128)(2,1)}, bf16[6,64,512]{2,1,0:T(8,128)(2,1)}, u32[]{:S(2)}, u32[]{:S(2)}) collective-permute-start(bf16[6,64,512]{2,1,0:T(8,128)(2,1)} %get-tuple-element.230), channel_id=1, source_target_pairs={{8,16},{12,20},{16,8},{20,12},{9,17},{13,21},{17,9},{21,13},{10,18... | collective-permute-start | bytes 1179656 | tf_op jit(solution)/shard_map/cond/branch_2_fun/ppermute | solution.py:519
  158.1 10.3 %collective-permute-start.58 = (bf16[6,64,512]{2,1,0:T(8,128)(2,1)}, bf16[6,64,512]{2,1,0:T(8,128)(2,1)}, u32[]{:S(2)}, u32[]{:S(2)}) collective-permute-start(bf16[6,64,512]{2,1,0:T(8,128)(2,1)} %get-tuple-element.363), channel_id=1, source_target_pairs={{0,8},{4,12},{16,24},{20,28},{8,0},{12,4},{24,16},{28,20},{1,9},{5... | collective-permute-start | bytes 1179656 | tf_op jit(solution)/shard_map/cond/branch_2_fun/while/body/ppermute | solution.py:519
  162.3 7.9 %collective-permute-start.59 = (bf16[6,64,512]{2,1,0:T(8,128)(2,1)}, bf16[6,64,512]{2,1,0:T(8,128)(2,1)}, u32[]{:S(2)}, u32[]{:S(2)}) collective-permute-start(bf16[6,64,512]{2,1,0:T(8,128)(2,1)} %get-tuple-element.364), channel_id=1, source_target_pairs={{8,16},{12,20},{16,8},{20,12},{9,17},{13,21},{17,9},{21,13},{10,18... | collective-permute-start | bytes 1179656 | tf_op jit(solution)/shard_map/cond/branch_2_fun/while/body/ppermute | solution.py:519
  178.9 1.1 copy-start.2
where the time goes:
time: 203 us; the launch traced here: 201 us
  starting transfers between devices  90.9 us (45%)
  Pallas kernels  76.5 us (38%)
  waiting for transfers between devices  14.4 us (7%)
  local copies, waits for them, and re-layouts  9.51 us (5%)
  blocking collectives  5.19 us (3%)
  loops' own time  2.35 us (1%)
  between operations  2.2 us (1%)
    ppermute x32, starting transfers between devices, swap(): swapped.append(lax.ppermute(sent, 'tbl', pairs))  85 us
    pallas_call x16, Pallas kernels, turn(): pl.pallas_call(functools.partial(turn_kernel, code, len(pieces), pool is...  49.6 us
    pallas_call x1, Pallas kernels, score(): pl.pallas_call(functools.partial(score_kernel, limits), out_shape=jax.Sha...  15.3 us
    ppermute x32, waiting for transfers between devices, swap(): swapped.append(lax.ppermute(sent, 'tbl', pairs))  11.7 us
    while x4, local copies, waits for them, and re-layouts  7.12 us
    ppermute x4, starting transfers between devices, piece(): return lax.ppermute(part, 'tbl', across)  5.97 us
    pallas_call x4, Pallas kernels, column_piece(): pl.pallas_call(functools.partial(piece_kernel, nodes, n), out_shape=jax.S...  5.28 us
    pallas_call x2, Pallas kernels, settle(): pl.pallas_call(settle_kernel, out_shape=jax.ShapeDtypeStruct(pool.shape,...  5.2 us
  transfers between devices with their start and end apart: 36, of which 8 were waited for; matrix products, arithmetic and copies ran while one was open for 3% of the time, Pallas kernels for 23%

commit v1 on v0

--- a/solution.py
+++ b/solution.py
@@ -56,6 +56,8 @@
             before = range(place - 1, -1, -1) if up else range(place + 1, nodes)
             pieces = piece_order(nodes, place)
             items = [(source, other, goal) for other in range(2) for goal in goals for source in (place, *before)]
+            if not before:
+                items.insert(len(goals) - 1, items.pop(len(goals)))
             end, here, segments = jnp.int32(0), {}, []
             for source, other, goal in items:
                 count, first, _ = rows[source, other]
@@ -423,7 +425,7 @@
     lax.fori_loop(0, count // LANES, gram_block, 0)
     for copy in weights:
         copy.wait()
-    step = 2 * LANES if count % (2 * LANES) == 0 else LANES
+    step = max(n * LANES for n in (1, 2, 4) if count % (n * LANES) == 0)
 
     def dense(hidden, weight, bias):
         product = jnp.dot(hidden, weight[...], preferred_element_type=jnp.float32)
@@ -436,7 +438,7 @@
         hidden = dense(hidden, w2, b2_ref)
         hidden = dense(hidden, w3, b3_ref)
         hidden = dense(hidden, w4, b4_ref)
-        final = lax.dot_general(wo_ref[...], hidden, (((1,), (1,)), ((), ())), preferred_element_type=jnp.float32)
+        final = lax.dot_general(wo_ref[...].reshape(1, wo_ref.shape[0]), hidden, (((1,), (1,)), ((), ())), preferred_element_type=jnp.float32)
         out_ref[:, lanes] = final[0:1] + bo_ref[0]
         return carry
 
@@ -447,7 +449,6 @@
     (w1, b1), (w2, b2), (w3, b3), (w4, b4), (wo, bo) = layers
     half, count = pool.shape[1:]
     rows = w1.shape[0]
-    wo = wo[None, :]
     anywhere = pl.BlockSpec(memory_space=pl.ANY)
     vmem = pl.BlockSpec(memory_space=pltpu.VMEM)
     flops = 2 * count * sum(w.size for w in (w1, w2, w3, w4))
@@ -469,7 +470,7 @@
                 pltpu.SemaphoreType.DMA((len(parts),)),
             ],
         ),
-        compiler_params=pltpu.CompilerParams(vmem_limit_bytes=20 << 20),
+        compiler_params=pltpu.CompilerParams(vmem_limit_bytes=60 << 20),
         cost_estimate=pl.CostEstimate(flops=flops, bytes_accessed=shards * half * count * 2, transcendentals=0),
         name="score",
     )(positions, pool, codes, piece, scales, *parts, bo)

time: 203 us -> 194 us (0.956)
  local copies, waits for them, and re-layouts: 9.51 us -> 2.71 us
  Pallas kernels: 76.5 us -> 70.4 us
  waiting for transfers between devices: 14.4 us -> 19.1 us
    while x4, local copies, waits for them, and re-layouts: 7.12 us -> 1.58 us
    ppermute x32, waiting for transfers between devices: 11.7 us -> 16.4 us  [swap(): swapped.append(lax.ppermute(sent, 'tbl', pairs))]
    pallas_call x16, Pallas kernels: 49.6 us -> 45.2 us  [turn(): pl.pallas_call(functools.partial(turn_kernel, code, len(pieces), pool is...]
  transfers between devices with their start and end apart: 36 -> 36, of which waited for: 8 -> 9; matrix products, arithmetic and copies ran while one was open for 3% -> 1% of each run, Pallas kernels for 23% -> 22%
where the time goes in v1:
time: 194 us; the launch traced here: 191 us
  starting transfers between devices  89.6 us (46%)
  Pallas kernels  70.4 us (36%)
  waiting for transfers between devices  19.1 us (10%)
  blocking collectives  5.33 us (3%)
  local copies, waits for them, and re-layouts  2.71 us (1%)
  loops' own time  2.11 us (1%)
    ppermute x32, starting transfers between devices, swap(): swapped.append(lax.ppermute(sent, 'tbl', pairs))  83.7 us
    pallas_call x16, Pallas kernels, turn(): pl.pallas_call(functools.partial(turn_kernel, code, len(pieces), pool is...  45.2 us
    ppermute x32, waiting for transfers between devices, swap(): swapped.append(lax.ppermute(sent, 'tbl', pairs))  16.4 us
    pallas_call x1, Pallas kernels, score(): pl.pallas_call(functools.partial(score_kernel, limits), out_shape=jax.Sha...  15.4 us
    ppermute x4, starting transfers between devices, piece(): return lax.ppermute(part, 'tbl', across)  5.85 us
    all_gather x1, blocking collectives, per_device(): return lax.all_gather(logits, 'pair', axis=0, tiled=True)  5.33 us
    pallas_call x2, Pallas kernels, settle(): pl.pallas_call(settle_kernel, out_shape=jax.ShapeDtypeStruct(pool.shape,...  4.56 us
    pallas_call x4, Pallas kernels, column_piece(): pl.pallas_call(functools.partial(piece_kernel, nodes, n), out_shape=jax.S...  4.14 us
  transfers between devices with their start and end apart: 36, of which 9 were waited for; matrix products, arithmetic and copies ran while one was open for 1% of the time, Pallas kernels for 22%

profile of v1, /device:TPU:0, one launch (start us, length us, event | category | flops | bytes accessed | tf_op | source)
XLA Modules:
  0.0 191.1 jit_solution(13798834951265649956)
XLA Ops:
  0.0 1.1 plan.1.pos_ref
  2.8 166.2 %conditional.1 = (bf16[236,64,512]{2,1,0:T(8,128)(2,1)}, bf16[14,64,512]{2,1,0:T(8,128)(2,1)}) conditional(s32[]{:T(128)} %clamp.3, (s32[]{:T(128)}, bf16[14,64,4096]{2,1,0:T(8,128)(2,1)}, f32[14,4096]{1,0:T(8,128)}, s32[8,256]{1,0:T(8,128)S(1)}) %tuple.22, (s32[]{:T(128)}, bf16[14,64,4096]{2,1,0:T(8,128)(2,1)}, ...), branch_computations={%region_0.0_spmd, %region_1.0_spmd, %region_2.0_spmd} | conditional | flops 8126468 | bytes 159778672 | solution.py:550
  3.1 3.0 %piece.20 = bf16[14,64,512]{2,1,0:T(8,128)(2,1)S(1)} custom-call(s32[1]{0:T(128)} %bitcast.3.me_ref, bf16[14,64,4096]{2,1,0:T(8,128)(2,1)} %get-tuple-element.373.codes_ref.refs_0_, f32[14,4096]{1,0:T(8,128)} %get-tuple-element.374.scales_ref.after_ref.refs_1_, f32[14,4096]{1,0:T(8,128)} %get-tuple-element.374.scales_ref.after_ref.refs_1_), custom_call_target="tpu_custom_call" | custom-call | flops 458752 | bytes 1835008 | tf_op jit(solution)/shard_map/cond/branch_2_fun/piece/pallas_call | solution.py:307
  6.1 3.1 %collective-permute-start.60 = (bf16[14,64,512]{2,1,0:T(8,128)(2,1)S(1)}, bf16[14,64,512]{2,1,0:T(8,128)(2,1)S(1)}, u32[]{:S(2)}, u32[]{:S(2)}) collective-permute-start(bf16[14,64,512]{2,1,0:T(8,128)(2,1)S(1)} %piece.20), channel_id=1, source_target_pairs={{0,4},{4,0},{8,12},{12,8},{16,20},{20,16},{24,28},{28,24},{1,5},{5... | collective-permute-start | bytes 2752520 | tf_op jit(solution)/shard_map/cond/branch_2_fun/ppermute | solution.py:515
  9.2 3.4 %turn.66 = (bf16[236,64,512]{2,1,0:T(8,128)(2,1)}, bf16[6,64,512]{2,1,0:T(8,128)(2,1)S(1)}, bf16[6,64,512]{2,1,0:T(8,128)(2,1)S(1)}) custom-call(s32[8,256]{1,0:T(8,128)S(1)} %get-tuple-element.372.table_ref, bf16[14,64,4096]{2,1,0:T(8,128)(2,1)} %get-tuple-element.373.codes_ref.refs_0_, f32[14,4096]{1,0:T(8,128)} %get-tuple-element.374.scales_ref.after_ref.refs_1_), custom_call_target="tpu_custom_call" | custom-call | flops 393216 | bytes 3145728 | tf_op jit(solution)/shard_map/cond/branch_2_fun/turn/pallas_call | solution.py:263
  12.6 1.4 collective-permute-start.61
  14.0 0.7 collective-permute-start.62
  14.7 1.6 turn.67
  16.3 5.2 %collective-permute-start.64 = (bf16[6,64,512]{2,1,0:T(8,128)(2,1)S(1)}, bf16[6,64,512]{2,1,0:T(8,128)(2,1)S(1)}, u32[]{:S(2)}, u32[]{:S(2)}) collective-permute-start(bf16[6,64,512]{2,1,0:T(8,128)(2,1)S(1)} %get-tuple-element.194), channel_id=1, source_target_pairs={{0,8},{4,12},{16,24},{20,28},{8,0},{12,4},{24,16},{28,20},{1,9},{5... | collective-permute-start | bytes 1179656 | tf_op jit(solution)/shard_map/cond/branch_2_fun/ppermute | solution.py:520
  21.5 0.7 collective-permute-start.65
  22.2 2.4 %collective-permute-done.61.refs_3_ = bf16[6,64,512]{2,1,0:T(8,128)(2,1)S(1)} collective-permute-done((bf16[6,64,512]{2,1,0:T(8,128)(2,1)S(1)}, bf16[6,64,512]{2,1,0:T(8,128)(2,1)S(1)}, u32[]{:S(2)}, u32[]{:S(2)}) %collective-permute-start.61) | collective-permute-done | bytes 393248 | tf_op jit(solution)/shard_map/cond/branch_2_fun/ppermute | solution.py:520
  24.6 2.5 %turn.68 = (bf16[236,64,512]{2,1,0:T(8,128)(2,1)}, bf16[6,64,512]{2,1,0:T(8,128)(2,1)S(1)}, bf16[6,64,512]{2,1,0:T(8,128)(2,1)S(1)}) custom-call(s32[8,256]{1,0:T(8,128)S(1)} %get-tuple-element.372.table_ref, bf16[14,64,4096]{2,1,0:T(8,128)(2,1)S(1)} %bitcast.23, f32[14,4096]{1,0:T(8,128)S(1)} %copy-done.2, ...), custom_call_target="tpu_custom_call", output_to_operand_aliasing={{0}: (3, {})} | custom-call | flops 393216 | bytes 3145728 | tf_op jit(solution)/shard_map/cond/branch_2_fun/turn/pallas_call | solution.py:263
  27.2 5.9 %collective-permute-start.66 = (bf16[6,64,512]{2,1,0:T(8,128)(2,1)S(1)}, bf16[6,64,512]{2,1,0:T(8,128)(2,1)S(1)}, u32[]{:S(2)}, u32[]{:S(2)}) collective-permute-start(bf16[6,64,512]{2,1,0:T(8,128)(2,1)S(1)} %get-tuple-element.192.after_ref), channel_id=1, source_target_pairs={{0,8},{4,12},{16,24},{20,28},{8,0},{12,4},{24,16},{28,20},{1,9},{5... | collective-permute-start | bytes 1179656 | tf_op jit(solution)/shard_map/cond/branch_2_fun/ppermute | solution.py:520
  33.6 0.7 collective-permute-start.67
  34.3 2.8 %turn.69 = (bf16[236,64,512]{2,1,0:T(8,128)(2,1)}, bf16[6,64,512]{2,1,0:T(8,128)(2,1)S(1)}, bf16[6,64,512]{2,1,0:T(8,128)(2,1)S(1)}) custom-call(s32[8,256]{1,0:T(8,128)S(1)} %get-tuple-element.372.table_ref, bf16[14,64,4096]{2,1,0:T(8,128)(2,1)S(1)} %bitcast.23, f32[14,4096]{1,0:T(8,128)S(1)} %copy-done.2, ...), custom_call_target="tpu_custom_call", output_to_operand_aliasing={{0}: (4, {})} | custom-call | flops 393216 | bytes 3145728 | tf_op jit(solution)/shard_map/cond/branch_2_fun/turn/pallas_call | solution.py:263
  37.1 4.0 %collective-permute-start.69 = (bf16[6,64,512]{2,1,0:T(8,128)(2,1)S(1)}, bf16[6,64,512]{2,1,0:T(8,128)(2,1)S(1)}, u32[]{:S(2)}, u32[]{:S(2)}) collective-permute-start(bf16[6,64,512]{2,1,0:T(8,128)(2,1)S(1)} %get-tuple-element.200), channel_id=1, source_target_pairs={{0,8},{4,12},{16,24},{20,28},{8,0},{12,4},{24,16},{28,20},{1,9},{5... | collective-permute-start | bytes 1179656 | tf_op jit(solution)/shard_map/cond/branch_2_fun/ppermute | solution.py:520
  41.1 3.0 %turn.70 = (bf16[236,64,512]{2,1,0:T(8,128)(2,1)}, bf16[6,64,512]{2,1,0:T(8,128)(2,1)S(1)}, bf16[6,64,512]{2,1,0:T(8,128)(2,1)S(1)}) custom-call(s32[8,256]{1,0:T(8,128)S(1)} %get-tuple-element.372.table_ref, bf16[14,64,4096]{2,1,0:T(8,128)(2,1)S(1)} %bitcast.23, f32[14,4096]{1,0:T(8,128)S(1)} %copy-done.2, ...), custom_call_target="tpu_custom_call", output_to_operand_aliasing={{0}: (4, {})} | custom-call | flops 393216 | bytes 3145728 | tf_op jit(solution)/shard_map/cond/branch_2_fun/turn/pallas_call | solution.py:263
  44.5 1.0 collective-permute-start.68
  45.5 0.7 collective-permute-start.70
  46.1 7.2 %collective-permute-start.71 = (bf16[6,64,512]{2,1,0:T(8,128)(2,1)S(1)}, bf16[6,64,512]{2,1,0:T(8,128)(2,1)S(1)}, u32[]{:S(2)}, u32[]{:S(2)}) collective-permute-start(bf16[6,64,512]{2,1,0:T(8,128)(2,1)S(1)} %get-tuple-element.198.after_ref), channel_id=1, source_target_pairs={{0,8},{4,12},{16,24},{20,28},{8,0},{12,4},{24,16},{28,20},{1,9},{5... | collective-permute-start | bytes 1179656 | tf_op jit(solution)/shard_map/cond/branch_2_fun/ppermute | solution.py:520
  53.3 0.7 collective-permute-start.72
  54.0 2.7 %collective-permute-done.63.refs_3_ = bf16[14,64,512]{2,1,0:T(8,128)(2,1)S(1)} collective-permute-done((bf16[14,64,512]{2,1,0:T(8,128)(2,1)S(1)}, bf16[14,64,512]{2,1,0:T(8,128)(2,1)S(1)}, u32[]{:S(2)}, u32[]{:S(2)}) %collective-permute-start.63) | collective-permute-done | bytes 917536 | tf_op jit(solution)/shard_map/cond/branch_2_fun/ppermute | solution.py:515
  56.8 2.9 %turn.71 = (bf16[236,64,512]{2,1,0:T(8,128)(2,1)}, bf16[6,64,512]{2,1,0:T(8,128)(2,1)S(1)}, bf16[6,64,512]{2,1,0:T(8,128)(2,1)S(1)}) custom-call(s32[8,256]{1,0:T(8,128)S(1)} %get-tuple-element.372.table_ref, bf16[14,64,4096]{2,1,0:T(8,128)(2,1)S(1)} %bitcast.23, f32[14,4096]{1,0:T(8,128)S(1)} %copy-done.2, ...), custom_call_target="tpu_custom_call", output_to_operand_aliasing={{0}: (5, {})} | custom-call | flops 393216 | bytes 3145728 | tf_op jit(solution)/shard_map/cond/branch_2_fun/turn/pallas_call | solution.py:263
  59.6 6.6 %collective-permute-start.73 = (bf16[6,64,512]{2,1,0:T(8,128)(2,1)S(1)}, bf16[6,64,512]{2,1,0:T(8,128)(2,1)S(1)}, u32[]{:S(2)}, u32[]{:S(2)}) collective-permute-start(bf16[6,64,512]{2,1,0:T(8,128)(2,1)S(1)} %get-tuple-element.205), channel_id=1, source_target_pairs={{0,8},{4,12},{16,24},{20,28},{8,0},{12,4},{24,16},{28,20},{1,9},{5... | collective-permute-start | bytes 1179656 | tf_op jit(solution)/shard_map/cond/branch_2_fun/ppermute | solution.py:520
  66.2 0.7 collective-permute-start.74
  66.9 2.5 %turn.72 = (bf16[236,64,512]{2,1,0:T(8,128)(2,1)}, bf16[6,64,512]{2,1,0:T(8,128)(2,1)S(1)}, bf16[6,64,512]{2,1,0:T(8,128)(2,1)S(1)}) custom-call(s32[8,256]{1,0:T(8,128)S(1)} %get-tuple-element.372.table_ref, bf16[14,64,4096]{2,1,0:T(8,128)(2,1)S(1)} %bitcast.23, f32[14,4096]{1,0:T(8,128)S(1)} %copy-done.2, ...), custom_call_target="tpu_custom_call", output_to_operand_aliasing={{0}: (5, {})} | custom-call | flops 393216 | bytes 3145728 | tf_op jit(solution)/shard_map/cond/branch_2_fun/turn/pallas_call | solution.py:263
  69.4 5.2 %collective-permute-start.75 = (bf16[6,64,512]{2,1,0:T(8,128)(2,1)S(1)}, bf16[6,64,512]{2,1,0:T(8,128)(2,1)S(1)}, u32[]{:S(2)}, u32[]{:S(2)}) collective-permute-start(bf16[6,64,512]{2,1,0:T(8,128)(2,1)S(1)} %get-tuple-element.208.after_ref), channel_id=1, source_target_pairs={{0,8},{4,12},{16,24},{20,28},{8,0},{12,4},{24,16},{28,20},{1,9},{5... | collective-permute-start | bytes 1179656 | tf_op jit(solution)/shard_map/cond/branch_2_fun/ppermute | solution.py:520
  74.7 0.7 collective-permute-start.76
  75.4 2.9 %turn.73 = (bf16[236,64,512]{2,1,0:T(8,128)(2,1)}, bf16[6,64,512]{2,1,0:T(8,128)(2,1)S(1)}, bf16[6,64,512]{2,1,0:T(8,128)(2,1)S(1)}) custom-call(s32[8,256]{1,0:T(8,128)S(1)} %get-tuple-element.372.table_ref, bf16[14,64,4096]{2,1,0:T(8,128)(2,1)S(1)} %bitcast.23, f32[14,4096]{1,0:T(8,128)S(1)} %copy-done.2, ...), custom_call_target="tpu_custom_call", output_to_operand_aliasing={{0}: (6, {})} | custom-call | flops 393216 | bytes 3145728 | tf_op jit(solution)/shard_map/cond/branch_2_fun/turn/pallas_call | solution.py:263
  78.3 5.6 %collective-permute-start.77 = (bf16[6,64,512]{2,1,0:T(8,128)(2,1)S(1)}, bf16[6,64,512]{2,1,0:T(8,128)(2,1)S(1)}, u32[]{:S(2)}, u32[]{:S(2)}) collective-permute-start(bf16[6,64,512]{2,1,0:T(8,128)(2,1)S(1)} %get-tuple-element.211), channel_id=1, source_target_pairs={{0,8},{4,12},{16,24},{20,28},{8,0},{12,4},{24,16},{28,20},{1,9},{5... | collective-permute-start | bytes 1179656 | tf_op jit(solution)/shard_map/cond/branch_2_fun/ppermute | solution.py:520
  83.9 0.7 collective-permute-start.78
  84.6 3.1 %turn.74 = (bf16[236,64,512]{2,1,0:T(8,128)(2,1)}, bf16[6,64,512]{2,1,0:T(8,128)(2,1)S(1)}, bf16[6,64,512]{2,1,0:T(8,128)(2,1)S(1)}) custom-call(s32[8,256]{1,0:T(8,128)S(1)} %get-tuple-element.372.table_ref, bf16[14,64,4096]{2,1,0:T(8,128)(2,1)S(1)} %bitcast.23, f32[14,4096]{1,0:T(8,128)S(1)} %copy-done.2, ...), custom_call_target="tpu_custom_call", output_to_operand_aliasing={{0}: (6, {})} | custom-call | flops 393216 | bytes 3145728 | tf_op jit(solution)/shard_map/cond/branch_2_fun/turn/pallas_call | solution.py:263
  87.7 4.5 %collective-permute-start.79 = (bf16[6,64,512]{2,1,0:T(8,128)(2,1)S(1)}, bf16[6,64,512]{2,1,0:T(8,128)(2,1)S(1)}, u32[]{:S(2)}, u32[]{:S(2)}) collective-permute-start(bf16[6,64,512]{2,1,0:T(8,128)(2,1)S(1)} %get-tuple-element.214), channel_id=1, source_target_pairs={{0,8},{4,12},{16,24},{20,28},{8,0},{12,4},{24,16},{28,20},{1,9},{5... | collective-permute-start | bytes 1179656 | tf_op jit(solution)/shard_map/cond/branch_2_fun/ppermute | solution.py:520
  92.2 0.7 collective-permute-start.80
  93.3 3.1 %turn.75 = (bf16[236,64,512]{2,1,0:T(8,128)(2,1)}, bf16[6,64,512]{2,1,0:T(8,128)(2,1)S(1)}, bf16[6,64,512]{2,1,0:T(8,128)(2,1)S(1)}) custom-call(s32[8,256]{1,0:T(8,128)S(1)} %get-tuple-element.372.table_ref, bf16[14,64,4096]{2,1,0:T(8,128)(2,1)S(1)} %bitcast.23, f32[14,4096]{1,0:T(8,128)S(1)} %copy-done.2, ...), custom_call_target="tpu_custom_call", output_to_operand_aliasing={{0}: (6, {})} | custom-call | flops 393216 | bytes 3145728 | tf_op jit(solution)/shard_map/cond/branch_2_fun/turn/pallas_call | solution.py:263
  96.4 4.5 %collective-permute-start.81 = (bf16[6,64,512]{2,1,0:T(8,128)(2,1)S(1)}, bf16[6,64,512]{2,1,0:T(8,128)(2,1)S(1)}, u32[]{:S(2)}, u32[]{:S(2)}) collective-permute-start(bf16[6,64,512]{2,1,0:T(8,128)(2,1)S(1)} %get-tuple-element.217), channel_id=1, source_target_pairs={{0,8},{4,12},{16,24},{20,28},{8,0},{12,4},{24,16},{28,20},{1,9},{5... | collective-permute-start | bytes 1179656 | tf_op jit(solution)/shard_map/cond/branch_2_fun/ppermute | solution.py:520
  100.9 0.7 collective-permute-start.82
  102.2 3.1 %turn.76 = (bf16[236,64,512]{2,1,0:T(8,128)(2,1)}, bf16[6,64,512]{2,1,0:T(8,128)(2,1)S(1)}, bf16[6,64,512]{2,1,0:T(8,128)(2,1)S(1)}) custom-call(s32[8,256]{1,0:T(8,128)S(1)} %get-tuple-element.372.table_ref, bf16[14,64,4096]{2,1,0:T(8,128)(2,1)S(1)} %bitcast.23, f32[14,4096]{1,0:T(8,128)S(1)} %copy-done.2, ...), custom_call_target="tpu_custom_call", output_to_operand_aliasing={{0}: (6, {})} | custom-call | flops 393216 | bytes 3145728 | tf_op jit(solution)/shard_map/cond/branch_2_fun/turn/pallas_call | solution.py:263
  105.3 3.9 %collective-permute-start.83 = (bf16[6,64,512]{2,1,0:T(8,128)(2,1)S(1)}, bf16[6,64,512]{2,1,0:T(8,128)(2,1)S(1)}, u32[]{:S(2)}, u32[]{:S(2)}) collective-permute-start(bf16[6,64,512]{2,1,0:T(8,128)(2,1)S(1)} %get-tuple-element.220), channel_id=1, source_target_pairs={{0,8},{4,12},{16,24},{20,28},{8,0},{12,4},{24,16},{28,20},{1,9},{5... | collective-permute-start | bytes 1179656 | tf_op jit(solution)/shard_map/cond/branch_2_fun/ppermute | solution.py:520
  109.2 0.7 collective-permute-start.84
  110.3 1.7 collective-permute-start.93
  112.0 3.1 %turn.77 = (bf16[236,64,512]{2,1,0:T(8,128)(2,1)}, bf16[6,64,512]{2,1,0:T(8,128)(2,1)S(1)}, bf16[6,64,512]{2,1,0:T(8,128)(2,1)S(1)}) custom-call(s32[8,256]{1,0:T(8,128)S(1)} %get-tuple-element.372.table_ref, bf16[14,64,4096]{2,1,0:T(8,128)(2,1)S(1)} %bitcast.23, f32[14,4096]{1,0:T(8,128)S(1)} %copy-done.2, ...), custom_call_target="tpu_custom_call", output_to_operand_aliasing={{0}: (6, {})} | custom-call | flops 393216 | bytes 3145728 | tf_op jit(solution)/shard_map/cond/branch_2_fun/turn/pallas_call | solution.py:263
  115.1 2.8 %collective-permute-start.85 = (bf16[6,64,512]{2,1,0:T(8,128)(2,1)S(1)}, bf16[6,64,512]{2,1,0:T(8,128)(2,1)S(1)}, u32[]{:S(2)}, u32[]{:S(2)}) collective-permute-start(bf16[6,64,512]{2,1,0:T(8,128)(2,1)S(1)} %get-tuple-element.223), channel_id=1, source_target_pairs={{0,8},{4,12},{16,24},{20,28},{8,0},{12,4},{24,16},{28,20},{1,9},{5... | collective-permute-start | bytes 1179656 | tf_op jit(solution)/shard_map/cond/branch_2_fun/ppermute | solution.py:520
  119.2 2.5 %turn.78 = (bf16[236,64,512]{2,1,0:T(8,128)(2,1)}, bf16[6,64,512]{2,1,0:T(8,128)(2,1)S(1)}, bf16[6,64,512]{2,1,0:T(8,128)(2,1)S(1)}) custom-call(s32[8,256]{1,0:T(8,128)S(1)} %get-tuple-element.372.table_ref, bf16[14,64,4096]{2,1,0:T(8,128)(2,1)S(1)} %bitcast.23, f32[14,4096]{1,0:T(8,128)S(1)} %copy-done.2, ...), custom_call_target="tpu_custom_call", output_to_operand_aliasing={{0}: (6, {})} | custom-call | flops 393216 | bytes 3145728 | tf_op jit(solution)/shard_map/cond/branch_2_fun/turn/pallas_call | solution.py:263
  121.7 4.6 %collective-permute-start.87 = (bf16[6,64,512]{2,1,0:T(8,128)(2,1)S(1)}, bf16[6,64,512]{2,1,0:T(8,128)(2,1)S(1)}, u32[]{:S(2)}, u32[]{:S(2)}) collective-permute-start(bf16[6,64,512]{2,1,0:T(8,128)(2,1)S(1)} %get-tuple-element.226), channel_id=1, source_target_pairs={{0,8},{4,12},{16,24},{20,28},{8,0},{12,4},{24,16},{28,20},{1,9},{5... | collective-permute-start | bytes 1179656 | tf_op jit(solution)/shard_map/cond/branch_2_fun/ppermute | solution.py:520
  127.0 2.5 %turn.79 = (bf16[236,64,512]{2,1,0:T(8,128)(2,1)}, bf16[6,64,512]{2,1,0:T(8,128)(2,1)S(1)}, bf16[6,64,512]{2,1,0:T(8,128)(2,1)S(1)}) custom-call(s32[8,256]{1,0:T(8,128)S(1)} %get-tuple-element.372.table_ref, bf16[14,64,4096]{2,1,0:T(8,128)(2,1)S(1)} %bitcast.23, f32[14,4096]{1,0:T(8,128)S(1)} %copy-done.2, ...), custom_call_target="tpu_custom_call", output_to_operand_aliasing={{0}: (6, {})} | custom-call | flops 393216 | bytes 3145728 | tf_op jit(solution)/shard_map/cond/branch_2_fun/turn/pallas_call | solution.py:263
  129.5 2.5 %collective-permute-done.87.refs_6_ = bf16[6,64,512]{2,1,0:T(8,128)(2,1)S(1)} collective-permute-done((bf16[6,64,512]{2,1,0:T(8,128)(2,1)S(1)}, bf16[6,64,512]{2,1,0:T(8,128)(2,1)S(1)}, u32[]{:S(2)}, u32[]{:S(2)}) %collective-permute-start.87) | collective-permute-done | bytes 393248 | tf_op jit(solution)/shard_map/cond/branch_2_fun/ppermute | solution.py:520
  132.1 2.5 %turn.80 = (bf16[236,64,512]{2,1,0:T(8,128)(2,1)}, bf16[6,64,512]{2,1,0:T(8,128)(2,1)S(1)}, bf16[6,64,512]{2,1,0:T(8,128)(2,1)S(1)}) custom-call(s32[8,256]{1,0:T(8,128)S(1)} %get-tuple-element.372.table_ref, bf16[14,64,4096]{2,1,0:T(8,128)(2,1)S(1)} %bitcast.23, f32[14,4096]{1,0:T(8,128)S(1)} %copy-done.2, ...), custom_call_target="tpu_custom_call", output_to_operand_aliasing={{0}: (6, {})} | custom-call | flops 393216 | bytes 3145728 | tf_op jit(solution)/shard_map/cond/branch_2_fun/turn/pallas_call | solution.py:263
  134.6 4.2 %collective-permute-start.91 = (bf16[6,64,512]{2,1,0:T(8,128)(2,1)S(1)}, bf16[6,64,512]{2,1,0:T(8,128)(2,1)S(1)}, u32[]{:S(2)}, u32[]{:S(2)}) collective-permute-start(bf16[6,64,512]{2,1,0:T(8,128)(2,1)S(1)} %get-tuple-element.231), channel_id=1, source_target_pairs={{0,8},{4,12},{16,24},{20,28},{8,0},{12,4},{24,16},{28,20},{1,9},{5... | collective-permute-start | bytes 1179656 | tf_op jit(solution)/shard_map/cond/branch_2_fun/ppermute | solution.py:520
  138.8 0.7 collective-permute-start.92
  139.5 2.8 %collective-permute-start.89 = (bf16[6,64,512]{2,1,0:T(8,128)(2,1)S(1)}, bf16[6,64,512]{2,1,0:T(8,128)(2,1)}, u32[]{:S(2)}, u32[]{:S(2)}) collective-permute-start(bf16[6,64,512]{2,1,0:T(8,128)(2,1)S(1)} %get-tuple-element.229), channel_id=1, source_target_pairs={{0,8},{4,12},{16,24},{20,28},{8,0},{12,4},{24,16},{28,20},{1,9},{5... | collective-permute-start | bytes 1179656 | tf_op jit(solution)/shard_map/cond/branch_2_fun/ppermute | solution.py:520
  142.3 1.4 collective-permute-start.90
  143.7 1.8 collective-permute-done.91
  145.5 4.3 %collective-permute-done.89 = bf16[6,64,512]{2,1,0:T(8,128)(2,1)} collective-permute-done((bf16[6,64,512]{2,1,0:T(8,128)(2,1)S(1)}, bf16[6,64,512]{2,1,0:T(8,128)(2,1)}, u32[]{:S(2)}, u32[]{:S(2)}) %collective-permute-start.89) | collective-permute-done | bytes 393248 | tf_op jit(solution)/shard_map/cond/branch_2_fun/ppermute | solution.py:520
  149.8 14.4 %while.17 = (s32[]{:T(128)}, bf16[236,64,512]{2,1,0:T(8,128)(2,1)}, bf16[6,64,512]{2,1,0:T(8,128)(2,1)}, bf16[6,64,512]{2,1,0:T(8,128)(2,1)}, bf16[6,64,512]{2,1...) while((s32[]{:T(128)}, bf16[236,64,512]{2,1,0:T(8,128)(2,1)}, ...), condition=%wide.region_4.0_spmd, body=%wide.region_3.0_spmd.sunk | while | flops 393218 | bytes 9437397 | solution.py:544
  150.4 3.7 %turn.81 = (bf16[236,64,512]{2,1,0:T(8,128)(2,1)}, bf16[6,64,512]{2,1,0:T(8,128)(2,1)S(1)}, bf16[6,64,512]{2,1,0:T(8,128)(2,1)S(1)}) custom-call(s32[8,256]{1,0:T(8,128)S(1)} %get-tuple-element.400.table_ref, s32[1]{0:T(128)} %bitcast.17.refs_0_, bf16[14,64,4096]{2,1,0:T(8,128)(2,1)} %get-tuple-element.401.refs_1_, ...), custom_call_target="tpu_custom_call", output_to_operand_aliasing={{0}: (7, {})} | custom-call | flops 393216 | bytes 3145728 | tf_op jit(solution)/shard_map/cond/branch_2_fun/while/body/turn/pallas_call | solution.py:263
  154.1 3.7 %collective-permute-start.58 = (bf16[6,64,512]{2,1,0:T(8,128)(2,1)S(1)}, bf16[6,64,512]{2,1,0:T(8,128)(2,1)S(1)}, u32[]{:S(2)}, u32[]{:S(2)}) collective-permute-start(bf16[6,64,512]{2,1,0:T(8,128)(2,1)S(1)} %get-tuple-element.363), channel_id=1, source_target_pairs={{0,8},{4,12},{16,24},{20,28},{8,0},{12,4},{24,16},{28,20},{1,9},{5... | collective-permute-start | bytes 1179656 | tf_op jit(solution)/shard_map/cond/branch_2_fun/while/body/ppermute | solution.py:520
  158.5 0.8 copy.117
  159.3 0.8 copy.118
  160.0 3.5 %collective-permute-done.58 = bf16[6,64,512]{2,1,0:T(8,128)(2,1)S(1)} collective-permute-done((bf16[6,64,512]{2,1,0:T(8,128)(2,1)S(1)}, bf16[6,64,512]{2,1,0:T(8,128)(2,1)S(1)}, u32[]{:S(2)}, u32[]{:S(2)}) %collective-permute-start.58) | collective-permute-done | bytes 393248 | tf_op jit(solution)/shard_map/cond/branch_2_fun/while/body/ppermute | solution.py:520
  164.3 2.6 %settle.10.pool_in = bf16[236,64,512]{2,1,0:T(8,128)(2,1)} custom-call(s32[8,256]{1,0:T(8,128)S(1)} %get-tuple-element.593, s32[1]{0:T(128)} %bitcast.5.round_ref, bf16[236,64,512]{2,1,0:T(8,128)(2,1)} %get-tuple-element.243.pool_in, bf16[6,64,512]{2,1,0:T(8,128)(2,1)} %get-tuple-element.244.recv_a, ...), custom_call_target="tpu_custom_call", output_to_operand_aliasing={{}: (2, {})} | custom-call | tf_op jit(solution)/shard_map/cond/branch_2_fun/settle/pallas_call | solution.py:341
  166.9 2.0 %settle.11 = bf16[236,64,512]{2,1,0:T(8,128)(2,1)} custom-call(s32[8,256]{1,0:T(8,128)S(1)} %get-tuple-element.593, s32[1]{0:T(128)} %bitcast.4.round_ref, bf16[236,64,512]{2,1,0:T(8,128)(2,1)} %settle.10.pool_in, bf16[6,64,512]{2,1,0:T(8,128)(2,1)S(1)} %get-tuple-element.246.recv_a, ...), custom_call_target="tpu_custom_call", output_to_operand_aliasing={{}: (2, {})} | custom-call | tf_op jit(solution)/shard_map/cond/branch_2_fun/settle/pallas_call | solution.py:341
  169.7 15.4 %score.1 = f32[1,512]{1,0:T(1,128)} custom-call(s32[8,256]{1,0:T(8,128)S(1)} %plan.1.pos_ref, bf16[236,64,512]{2,1,0:T(8,128)(2,1)} %get-tuple-element.251.pool_ref, bf16[14,64,4096]{2,1,0:T(8,128)(2,1)} %codes_ref.1, bf16[14,64,512]{2,1,0:T(8,128)(2,1)} %get-tuple-element.252.piece_ref, f32[14,4096]{1,0:T(8,128)} %scales_ref.1, bf16[351,1024]{1,0:T(8,128)(2,1)} %refs_0_.1, ...), custom_call_target="tpu_custom_call" | custom-call | flops 2112880640 | bytes 3538944 | tf_op jit(solution)/shard_map/score/pallas_call | solution.py:456
  185.1 5.3 %all-gather = f32[4,1,512]{2,1,0:T(1,128)S(1)} all-gather(f32[1,1,512]{2,1,0:T(1,128)} %bitcast.24), channel_id=1, replica_groups=mesh['tbl'=8,'pair'=4] {'pair'}, dimensions={0}, use_global_device_ids=true | all-gather | bytes 10240 | tf_op jit(solution)/shard_map/all_gather | solution.py:567
  (54 shorter events, 6.2 us)
Async XLA Ops:
  3.0 11.6 %slice-start.4 = ((s8[7340032]{0:T(1024)(128)(4,1)}), s8[4194304]{0:T(1024)(128)(4,1)S(1)}, s32[]{:S(2)}) async-start(s8[7340032]{0:T(1024)(128)(4,1)} %bitcast.22), calls=%async_computation.4 | async-start | bytes 8388608 | tf_op jit(solution)/shard_map/cond
  3.0 11.6 %copy-start.2 = (f32[14,4096]{1,0:T(8,128)S(1)}, f32[14,4096]{1,0:T(8,128)}, u32[]{:S(2)}) copy-start(f32[14,4096]{1,0:T(8,128)} %get-tuple-element.374.scales_ref.after_ref.refs_1_) | copy-start | bytes 688132 | tf_op jit(solution)/shard_map/cond
  3.0 11.6 %slice-start.5 = ((s8[7340032]{0:T(1024)(128)(4,1)}), s8[3145728]{0:T(1024)(128)(4,1)S(1)}, s32[]{:S(2)}) async-start(s8[7340032]{0:T(1024)(128)(4,1)} %bitcast.22), calls=%async_computation.5 | async-start | bytes 6291456 | tf_op jit(solution)/shard_map/cond
  6.1 28.2 %collective-permute-start.60 = (bf16[14,64,512]{2,1,0:T(8,128)(2,1)S(1)}, bf16[14,64,512]{2,1,0:T(8,128)(2,1)S(1)}, u32[]{:S(2)}, u32[]{:S(2)}) collective-permute-start(bf16[14,64,512]{2,1,0:T(8,128)(2,1)S(1)} %piece.20), channel_id=1, source_target_pairs={{0,4},{4,0},{8,12},{12,8},{16,20},{20,16},{24,28},{28,24},{1,5},{5... | collective-permute-start | bytes 2752520 | tf_op jit(solution)/shard_map/cond/branch_2_fun/ppermute | solution.py:515
  12.6 12.1 %collective-permute-start.61 = (bf16[6,64,512]{2,1,0:T(8,128)(2,1)S(1)}, bf16[6,64,512]{2,1,0:T(8,128)(2,1)S(1)}, u32[]{:S(2)}, u32[]{:S(2)}) collective-permute-start(bf16[6,64,512]{2,1,0:T(8,128)(2,1)S(1)} %get-tuple-element.190), channel_id=1, source_target_pairs={{0,8},{4,12},{16,24},{20,28},{8,0},{12,4},{24,16},{28,20},{1,9},{5... | collective-permute-start | bytes 1179656 | tf_op jit(solution)/shard_map/cond/branch_2_fun/ppermute | solution.py:520
  14.0 10.7 %collective-permute-start.62 = (bf16[6,64,512]{2,1,0:T(8,128)(2,1)S(1)}, bf16[6,64,512]{2,1,0:T(8,128)(2,1)S(1)}, u32[]{:S(2)}, u32[]{:S(2)}) collective-permute-start(bf16[6,64,512]{2,1,0:T(8,128)(2,1)S(1)} %get-tuple-element.191), channel_id=1, source_target_pairs={{8,16},{12,20},{16,8},{20,12},{9,17},{13,21},{17,9},{21,13},{10,18... | collective-permute-start | bytes 1179656 | tf_op jit(solution)/shard_map/cond/branch_2_fun/ppermute | solution.py:520
  16.3 17.3 %collective-permute-start.64 = (bf16[6,64,512]{2,1,0:T(8,128)(2,1)S(1)}, bf16[6,64,512]{2,1,0:T(8,128)(2,1)S(1)}, u32[]{:S(2)}, u32[]{:S(2)}) collective-permute-start(bf16[6,64,512]{2,1,0:T(8,128)(2,1)S(1)} %get-tuple-element.194), channel_id=1, source_target_pairs={{0,8},{4,12},{16,24},{20,28},{8,0},{12,4},{24,16},{28,20},{1,9},{5... | collective-permute-start | bytes 1179656 | tf_op jit(solution)/shard_map/cond/branch_2_fun/ppermute | solution.py:520
  21.5 12.7 %collective-permute-start.65 = (bf16[6,64,512]{2,1,0:T(8,128)(2,1)S(1)}, bf16[6,64,512]{2,1,0:T(8,128)(2,1)S(1)}, u32[]{:S(2)}, u32[]{:S(2)}) collective-permute-start(bf16[6,64,512]{2,1,0:T(8,128)(2,1)S(1)} %get-tuple-element.195), channel_id=1, source_target_pairs={{8,16},{12,20},{16,8},{20,12},{9,17},{13,21},{17,9},{21,13},{10,18... | collective-permute-start | bytes 1179656 | tf_op jit(solution)/shard_map/cond/branch_2_fun/ppermute | solution.py:520
  27.2 13.9 %collective-permute-start.66 = (bf16[6,64,512]{2,1,0:T(8,128)(2,1)S(1)}, bf16[6,64,512]{2,1,0:T(8,128)(2,1)S(1)}, u32[]{:S(2)}, u32[]{:S(2)}) collective-permute-start(bf16[6,64,512]{2,1,0:T(8,128)(2,1)S(1)} %get-tuple-element.192.after_ref), channel_id=1, source_target_pairs={{0,8},{4,12},{16,24},{20,28},{8,0},{12,4},{24,16},{28,20},{1,9},{5... | collective-permute-start | bytes 1179656 | tf_op jit(solution)/shard_map/cond/branch_2_fun/ppermute | solution.py:520
  33.5 23.3 %collective-permute-start.63 = (bf16[14,64,512]{2,1,0:T(8,128)(2,1)S(1)}, bf16[14,64,512]{2,1,0:T(8,128)(2,1)S(1)}, u32[]{:S(2)}, u32[]{:S(2)}) collective-permute-start(bf16[14,64,512]{2,1,0:T(8,128)(2,1)S(1)} %piece.21), channel_id=1, source_target_pairs={{0,4},{4,0},{8,12},{12,8},{16,20},{20,16},{24,28},{28,24},{1,5},{5... | collective-permute-start | bytes 2752520 | tf_op jit(solution)/shard_map/cond/branch_2_fun/ppermute | solution.py:515
  33.6 7.5 %collective-permute-start.67 = (bf16[6,64,512]{2,1,0:T(8,128)(2,1)S(1)}, bf16[6,64,512]{2,1,0:T(8,128)(2,1)S(1)}, u32[]{:S(2)}, u32[]{:S(2)}) collective-permute-start(bf16[6,64,512]{2,1,0:T(8,128)(2,1)S(1)} %get-tuple-element.197), channel_id=1, source_target_pairs={{8,16},{12,20},{16,8},{20,12},{9,17},{13,21},{17,9},{21,13},{10,18... | collective-permute-start | bytes 1179656 | tf_op jit(solution)/shard_map/cond/branch_2_fun/ppermute | solution.py:520
  34.3 97.8 %copy-start.3 = (bf16[14,64,512]{2,1,0:T(8,128)(2,1)}, bf16[14,64,512]{2,1,0:T(8,128)(2,1)S(1)}, u32[]{:S(2)}) copy-start(bf16[14,64,512]{2,1,0:T(8,128)(2,1)S(1)} %collective-permute-done.60.refs_2_) | copy-start | bytes 2752516 | tf_op jit(solution)/shard_map/cond
  37.1 16.2 %collective-permute-start.69 = (bf16[6,64,512]{2,1,0:T(8,128)(2,1)S(1)}, bf16[6,64,512]{2,1,0:T(8,128)(2,1)S(1)}, u32[]{:S(2)}, u32[]{:S(2)}) collective-permute-start(bf16[6,64,512]{2,1,0:T(8,128)(2,1)S(1)} %get-tuple-element.200), channel_id=1, source_target_pairs={{0,8},{4,12},{16,24},{20,28},{8,0},{12,4},{24,16},{28,20},{1,9},{5... | collective-permute-start | bytes 1179656 | tf_op jit(solution)/shard_map/cond/branch_2_fun/ppermute | solution.py:520
  44.5 30.9 %collective-permute-start.68 = (bf16[14,64,512]{2,1,0:T(8,128)(2,1)S(1)}, bf16[14,64,512]{2,1,0:T(8,128)(2,1)S(1)}, u32[]{:S(2)}, u32[]{:S(2)}) collective-permute-start(bf16[14,64,512]{2,1,0:T(8,128)(2,1)S(1)} %piece.22), channel_id=1, source_target_pairs={{0,4},{4,0},{8,12},{12,8},{16,20},{20,16},{24,28},{28,24},{1,5},{5... | collective-permute-start | bytes 2752520 | tf_op jit(solution)/shard_map/cond/branch_2_fun/ppermute | solution.py:515
  45.5 8.6 %collective-permute-start.70 = (bf16[6,64,512]{2,1,0:T(8,128)(2,1)S(1)}, bf16[6,64,512]{2,1,0:T(8,128)(2,1)S(1)}, u32[]{:S(2)}, u32[]{:S(2)}) collective-permute-start(bf16[6,64,512]{2,1,0:T(8,128)(2,1)S(1)} %get-tuple-element.201), channel_id=1, source_target_pairs={{8,16},{12,20},{16,8},{20,12},{9,17},{13,21},{17,9},{21,13},{10,18... | collective-permute-start | bytes 1179656 | tf_op jit(solution)/shard_map/cond/branch_2_fun/ppermute | solution.py:520
  46.1 20.8 %collective-permute-start.71 = (bf16[6,64,512]{2,1,0:T(8,128)(2,1)S(1)}, bf16[6,64,512]{2,1,0:T(8,128)(2,1)S(1)}, u32[]{:S(2)}, u32[]{:S(2)}) collective-permute-start(bf16[6,64,512]{2,1,0:T(8,128)(2,1)S(1)} %get-tuple-element.198.after_ref), channel_id=1, source_target_pairs={{0,8},{4,12},{16,24},{20,28},{8,0},{12,4},{24,16},{28,20},{1,9},{5... | collective-permute-start | bytes 1179656 | tf_op jit(solution)/shard_map/cond/branch_2_fun/ppermute | solution.py:520
  53.3 13.6 %collective-permute-start.72 = (bf16[6,64,512]{2,1,0:T(8,128)(2,1)S(1)}, bf16[6,64,512]{2,1,0:T(8,128)(2,1)S(1)}, u32[]{:S(2)}, u32[]{:S(2)}) collective-permute-start(bf16[6,64,512]{2,1,0:T(8,128)(2,1)S(1)} %get-tuple-element.203), channel_id=1, source_target_pairs={{8,16},{12,20},{16,8},{20,12},{9,17},{13,21},{17,9},{21,13},{10,18... | collective-permute-start | bytes 1179656 | tf_op jit(solution)/shard_map/cond/branch_2_fun/ppermute | solution.py:520
  56.8 75.3 %copy-start.4 = (bf16[14,64,512]{2,1,0:T(8,128)(2,1)}, bf16[14,64,512]{2,1,0:T(8,128)(2,1)S(1)}, u32[]{:S(2)}) copy-start(bf16[14,64,512]{2,1,0:T(8,128)(2,1)S(1)} %collective-permute-done.63.refs_3_) | copy-start | bytes 2752516 | tf_op jit(solution)/shard_map/cond
  59.6 15.7 %collective-permute-start.73 = (bf16[6,64,512]{2,1,0:T(8,128)(2,1)S(1)}, bf16[6,64,512]{2,1,0:T(8,128)(2,1)S(1)}, u32[]{:S(2)}, u32[]{:S(2)}) collective-permute-start(bf16[6,64,512]{2,1,0:T(8,128)(2,1)S(1)} %get-tuple-element.205), channel_id=1, source_target_pairs={{0,8},{4,12},{16,24},{20,28},{8,0},{12,4},{24,16},{28,20},{1,9},{5... | collective-permute-start | bytes 1179656 | tf_op jit(solution)/shard_map/cond/branch_2_fun/ppermute | solution.py:520
  66.2 9.2 %collective-permute-start.74 = (bf16[6,64,512]{2,1,0:T(8,128)(2,1)S(1)}, bf16[6,64,512]{2,1,0:T(8,128)(2,1)S(1)}, u32[]{:S(2)}, u32[]{:S(2)}) collective-permute-start(bf16[6,64,512]{2,1,0:T(8,128)(2,1)S(1)} %get-tuple-element.206), channel_id=1, source_target_pairs={{8,16},{12,20},{16,8},{20,12},{9,17},{13,21},{17,9},{21,13},{10,18... | collective-permute-start | bytes 1179656 | tf_op jit(solution)/shard_map/cond/branch_2_fun/ppermute | solution.py:520
  69.4 15.2 %collective-permute-start.75 = (bf16[6,64,512]{2,1,0:T(8,128)(2,1)S(1)}, bf16[6,64,512]{2,1,0:T(8,128)(2,1)S(1)}, u32[]{:S(2)}, u32[]{:S(2)}) collective-permute-start(bf16[6,64,512]{2,1,0:T(8,128)(2,1)S(1)} %get-tuple-element.208.after_ref), channel_id=1, source_target_pairs={{0,8},{4,12},{16,24},{20,28},{8,0},{12,4},{24,16},{28,20},{1,9},{5... | collective-permute-start | bytes 1179656 | tf_op jit(solution)/shard_map/cond/branch_2_fun/ppermute | solution.py:520
  74.7 9.9 %collective-permute-start.76 = (bf16[6,64,512]{2,1,0:T(8,128)(2,1)S(1)}, bf16[6,64,512]{2,1,0:T(8,128)(2,1)S(1)}, u32[]{:S(2)}, u32[]{:S(2)}) collective-permute-start(bf16[6,64,512]{2,1,0:T(8,128)(2,1)S(1)} %get-tuple-element.209), channel_id=1, source_target_pairs={{8,16},{12,20},{16,8},{20,12},{9,17},{13,21},{17,9},{21,13},{10,18... | collective-permute-start | bytes 1179656 | tf_op jit(solution)/shard_map/cond/branch_2_fun/ppermute | solution.py:520
  75.4 56.7 %copy-start.5 = (bf16[14,64,512]{2,1,0:T(8,128)(2,1)}, bf16[14,64,512]{2,1,0:T(8,128)(2,1)S(1)}, u32[]{:S(2)}) copy-start(bf16[14,64,512]{2,1,0:T(8,128)(2,1)S(1)} %collective-permute-done.68.refs_4_) | copy-start | bytes 2752516 | tf_op jit(solution)/shard_map/cond
  78.3 15.0 %collective-permute-start.77 = (bf16[6,64,512]{2,1,0:T(8,128)(2,1)S(1)}, bf16[6,64,512]{2,1,0:T(8,128)(2,1)S(1)}, u32[]{:S(2)}, u32[]{:S(2)}) collective-permute-start(bf16[6,64,512]{2,1,0:T(8,128)(2,1)S(1)} %get-tuple-element.211), channel_id=1, source_target_pairs={{0,8},{4,12},{16,24},{20,28},{8,0},{12,4},{24,16},{28,20},{1,9},{5... | collective-permute-start | bytes 1179656 | tf_op jit(solution)/shard_map/cond/branch_2_fun/ppermute | solution.py:520
  83.9 9.4 %collective-permute-start.78 = (bf16[6,64,512]{2,1,0:T(8,128)(2,1)S(1)}, bf16[6,64,512]{2,1,0:T(8,128)(2,1)S(1)}, u32[]{:S(2)}, u32[]{:S(2)}) collective-permute-start(bf16[6,64,512]{2,1,0:T(8,128)(2,1)S(1)} %get-tuple-element.212), channel_id=1, source_target_pairs={{8,16},{12,20},{16,8},{20,12},{9,17},{13,21},{17,9},{21,13},{10,18... | collective-permute-start | bytes 1179656 | tf_op jit(solution)/shard_map/cond/branch_2_fun/ppermute | solution.py:520
  87.7 14.5 %collective-permute-start.79 = (bf16[6,64,512]{2,1,0:T(8,128)(2,1)S(1)}, bf16[6,64,512]{2,1,0:T(8,128)(2,1)S(1)}, u32[]{:S(2)}, u32[]{:S(2)}) collective-permute-start(bf16[6,64,512]{2,1,0:T(8,128)(2,1)S(1)} %get-tuple-element.214), channel_id=1, source_target_pairs={{0,8},{4,12},{16,24},{20,28},{8,0},{12,4},{24,16},{28,20},{1,9},{5... | collective-permute-start | bytes 1179656 | tf_op jit(solution)/shard_map/cond/branch_2_fun/ppermute | solution.py:520
  92.2 10.0 %collective-permute-start.80 = (bf16[6,64,512]{2,1,0:T(8,128)(2,1)S(1)}, bf16[6,64,512]{2,1,0:T(8,128)(2,1)S(1)}, u32[]{:S(2)}, u32[]{:S(2)}) collective-permute-start(bf16[6,64,512]{2,1,0:T(8,128)(2,1)S(1)} %get-tuple-element.215), channel_id=1, source_target_pairs={{8,16},{12,20},{16,8},{20,12},{9,17},{13,21},{17,9},{21,13},{10,18... | collective-permute-start | bytes 1179656 | tf_op jit(solution)/shard_map/cond/branch_2_fun/ppermute | solution.py:520
  96.4 15.6 %collective-permute-start.81 = (bf16[6,64,512]{2,1,0:T(8,128)(2,1)S(1)}, bf16[6,64,512]{2,1,0:T(8,128)(2,1)S(1)}, u32[]{:S(2)}, u32[]{:S(2)}) collective-permute-start(bf16[6,64,512]{2,1,0:T(8,128)(2,1)S(1)} %get-tuple-element.217), channel_id=1, source_target_pairs={{0,8},{4,12},{16,24},{20,28},{8,0},{12,4},{24,16},{28,20},{1,9},{5... | collective-permute-start | bytes 1179656 | tf_op jit(solution)/shard_map/cond/branch_2_fun/ppermute | solution.py:520
  100.9 11.1 %collective-permute-start.82 = (bf16[6,64,512]{2,1,0:T(8,128)(2,1)S(1)}, bf16[6,64,512]{2,1,0:T(8,128)(2,1)S(1)}, u32[]{:S(2)}, u32[]{:S(2)}) collective-permute-start(bf16[6,64,512]{2,1,0:T(8,128)(2,1)S(1)} %get-tuple-element.218), channel_id=1, source_target_pairs={{8,16},{12,20},{16,8},{20,12},{9,17},{13,21},{17,9},{21,13},{10,18... | collective-permute-start | bytes 1179656 | tf_op jit(solution)/shard_map/cond/branch_2_fun/ppermute | solution.py:520
  105.3 13.9 %collective-permute-start.83 = (bf16[6,64,512]{2,1,0:T(8,128)(2,1)S(1)}, bf16[6,64,512]{2,1,0:T(8,128)(2,1)S(1)}, u32[]{:S(2)}, u32[]{:S(2)}) collective-permute-start(bf16[6,64,512]{2,1,0:T(8,128)(2,1)S(1)} %get-tuple-element.220), channel_id=1, source_target_pairs={{0,8},{4,12},{16,24},{20,28},{8,0},{12,4},{24,16},{28,20},{1,9},{5... | collective-permute-start | bytes 1179656 | tf_op jit(solution)/shard_map/cond/branch_2_fun/ppermute | solution.py:520
  109.2 10.0 %collective-permute-start.84 = (bf16[6,64,512]{2,1,0:T(8,128)(2,1)S(1)}, bf16[6,64,512]{2,1,0:T(8,128)(2,1)S(1)}, u32[]{:S(2)}, u32[]{:S(2)}) collective-permute-start(bf16[6,64,512]{2,1,0:T(8,128)(2,1)S(1)} %get-tuple-element.221), channel_id=1, source_target_pairs={{8,16},{12,20},{16,8},{20,12},{9,17},{13,21},{17,9},{21,13},{10,18... | collective-permute-start | bytes 1179656 | tf_op jit(solution)/shard_map/cond/branch_2_fun/ppermute | solution.py:520
  110.3 33.4 %collective-permute-start.93 = (bf16[14,64,512]{2,1,0:T(8,128)(2,1)S(1)}, bf16[14,64,512]{2,1,0:T(8,128)(2,1)}, u32[]{:S(2)}, u32[]{:S(2)}) collective-permute-start(bf16[14,64,512]{2,1,0:T(8,128)(2,1)S(1)} %piece.23), channel_id=1, source_target_pairs={{0,4},{4,0},{8,12},{12,8},{16,20},{20,16},{24,28},{28,24},{1,5},{5... | collective-permute-start | bytes 2752520 | tf_op jit(solution)/shard_map/cond/branch_2_fun/ppermute | solution.py:515
  115.1 11.9 %collective-permute-start.85 = (bf16[6,64,512]{2,1,0:T(8,128)(2,1)S(1)}, bf16[6,64,512]{2,1,0:T(8,128)(2,1)S(1)}, u32[]{:S(2)}, u32[]{:S(2)}) collective-permute-start(bf16[6,64,512]{2,1,0:T(8,128)(2,1)S(1)} %get-tuple-element.223), channel_id=1, source_target_pairs={{0,8},{4,12},{16,24},{20,28},{8,0},{12,4},{24,16},{28,20},{1,9},{5... | collective-permute-start | bytes 1179656 | tf_op jit(solution)/shard_map/cond/branch_2_fun/ppermute | solution.py:520
  117.9 9.1 %collective-permute-start.86 = (bf16[6,64,512]{2,1,0:T(8,128)(2,1)S(1)}, bf16[6,64,512]{2,1,0:T(8,128)(2,1)S(1)}, u32[]{:S(2)}, u32[]{:S(2)}) collective-permute-start(bf16[6,64,512]{2,1,0:T(8,128)(2,1)S(1)} %get-tuple-element.224), channel_id=1, source_target_pairs={{8,16},{12,20},{16,8},{20,12},{9,17},{13,21},{17,9},{21,13},{10,18... | collective-permute-start | bytes 1179656 | tf_op jit(solution)/shard_map/cond/branch_2_fun/ppermute | solution.py:520
  121.7 10.3 %collective-permute-start.87 = (bf16[6,64,512]{2,1,0:T(8,128)(2,1)S(1)}, bf16[6,64,512]{2,1,0:T(8,128)(2,1)S(1)}, u32[]{:S(2)}, u32[]{:S(2)}) collective-permute-start(bf16[6,64,512]{2,1,0:T(8,128)(2,1)S(1)} %get-tuple-element.226), channel_id=1, source_target_pairs={{0,8},{4,12},{16,24},{20,28},{8,0},{12,4},{24,16},{28,20},{1,9},{5... | collective-permute-start | bytes 1179656 | tf_op jit(solution)/shard_map/cond/branch_2_fun/ppermute | solution.py:520
  126.3 5.8 %collective-permute-start.88 = (bf16[6,64,512]{2,1,0:T(8,128)(2,1)S(1)}, bf16[6,64,512]{2,1,0:T(8,128)(2,1)S(1)}, u32[]{:S(2)}, u32[]{:S(2)}) collective-permute-start(bf16[6,64,512]{2,1,0:T(8,128)(2,1)S(1)} %get-tuple-element.227), channel_id=1, source_target_pairs={{8,16},{12,20},{16,8},{20,12},{9,17},{13,21},{17,9},{21,13},{10,18... | collective-permute-start | bytes 1179656 | tf_op jit(solution)/shard_map/cond/branch_2_fun/ppermute | solution.py:520
  134.6 10.9 %collective-permute-start.91 = (bf16[6,64,512]{2,1,0:T(8,128)(2,1)S(1)}, bf16[6,64,512]{2,1,0:T(8,128)(2,1)S(1)}, u32[]{:S(2)}, u32[]{:S(2)}) collective-permute-start(bf16[6,64,512]{2,1,0:T(8,128)(2,1)S(1)} %get-tuple-element.231), channel_id=1, source_target_pairs={{0,8},{4,12},{16,24},{20,28},{8,0},{12,4},{24,16},{28,20},{1,9},{5... | collective-permute-start | bytes 1179656 | tf_op jit(solution)/shard_map/cond/branch_2_fun/ppermute | solution.py:520
  138.8 6.7 %collective-permute-start.92 = (bf16[6,64,512]{2,1,0:T(8,128)(2,1)S(1)}, bf16[6,64,512]{2,1,0:T(8,128)(2,1)S(1)}, u32[]{:S(2)}, u32[]{:S(2)}) collective-permute-start(bf16[6,64,512]{2,1,0:T(8,128)(2,1)S(1)} %get-tuple-element.232), channel_id=1, source_target_pairs={{8,16},{12,20},{16,8},{20,12},{9,17},{13,21},{17,9},{21,13},{10,18... | collective-permute-start | bytes 1179656 | tf_op jit(solution)/shard_map/cond/branch_2_fun/ppermute | solution.py:520
  139.5 10.3 %collective-permute-start.89 = (bf16[6,64,512]{2,1,0:T(8,128)(2,1)S(1)}, bf16[6,64,512]{2,1,0:T(8,128)(2,1)}, u32[]{:S(2)}, u32[]{:S(2)}) collective-permute-start(bf16[6,64,512]{2,1,0:T(8,128)(2,1)S(1)} %get-tuple-element.229), channel_id=1, source_target_pairs={{0,8},{4,12},{16,24},{20,28},{8,0},{12,4},{24,16},{28,20},{1,9},{5... | collective-permute-start | bytes 1179656 | tf_op jit(solution)/shard_map/cond/branch_2_fun/ppermute | solution.py:520
  142.3 7.6 %collective-permute-start.90 = (bf16[6,64,512]{2,1,0:T(8,128)(2,1)S(1)}, bf16[6,64,512]{2,1,0:T(8,128)(2,1)}, u32[]{:S(2)}, u32[]{:S(2)}) collective-permute-start(bf16[6,64,512]{2,1,0:T(8,128)(2,1)S(1)} %get-tuple-element.230), channel_id=1, source_target_pairs={{8,16},{12,20},{16,8},{20,12},{9,17},{13,21},{17,9},{21,13},{10,18... | collective-permute-start | bytes 1179656 | tf_op jit(solution)/shard_map/cond/branch_2_fun/ppermute | solution.py:520
  154.1 9.5 %collective-permute-start.58 = (bf16[6,64,512]{2,1,0:T(8,128)(2,1)S(1)}, bf16[6,64,512]{2,1,0:T(8,128)(2,1)S(1)}, u32[]{:S(2)}, u32[]{:S(2)}) collective-permute-start(bf16[6,64,512]{2,1,0:T(8,128)(2,1)S(1)} %get-tuple-element.363), channel_id=1, source_target_pairs={{0,8},{4,12},{16,24},{20,28},{8,0},{12,4},{24,16},{28,20},{1,9},{5... | collective-permute-start | bytes 1179656 | tf_op jit(solution)/shard_map/cond/branch_2_fun/while/body/ppermute | solution.py:520
  157.8 5.8 %collective-permute-start.59 = (bf16[6,64,512]{2,1,0:T(8,128)(2,1)S(1)}, bf16[6,64,512]{2,1,0:T(8,128)(2,1)S(1)}, u32[]{:S(2)}, u32[]{:S(2)}) collective-permute-start(bf16[6,64,512]{2,1,0:T(8,128)(2,1)S(1)} %get-tuple-element.364), channel_id=1, source_target_pairs={{8,16},{12,20},{16,8},{20,12},{9,17},{13,21},{17,9},{21,13},{10,18... | collective-permute-start | bytes 1179656 | tf_op jit(solution)/shard_map/cond/branch_2_fun/while/body/ppermute | solution.py:520
